TPU v7x, 32 devices: a whole 2x2x4 slice. The times are simulated.
32 devices in a mesh: seq: 4 (over x, core), fsdp: 8 (over z, y).
Axes of the slice: x: 2, y: 2, z: 4, core: 2. Of those that a mesh axis runs over, the one named last changes fastest.
Arguments:
- inputs: bfloat16 [16, 2048, 768], P('fsdp', 'seq'), may hold values from -6 to 6
- segment_ids: int32 [16, 1024], P('fsdp'), may hold values from 0 to 15, as said below
- block_ids: int32 [16, 1024], P('fsdp'), may hold values from 0 to 31, as said below
- attn_gain: bfloat16 [768], P('fsdp'), may hold values from 0.099609375 to 1.8984375
- attn_shift: bfloat16 [768], P('fsdp'), may hold values from -3 to 3
- proj_in: bfloat16 [768, 2304], P('fsdp'), may hold values from -0.21875 to 0.21875
- bias_in: bfloat16 [2304], P('fsdp'), may hold values from -2 to 2
- proj_out: bfloat16 [768, 768], P('fsdp'), may hold values from -0.875 to 0.875
- bias_out: bfloat16 [768], P('fsdp'), may hold values from -2 to 2
- mlp_gain: bfloat16 [768], P('fsdp'), may hold values from 0.099609375 to 1.8984375
- mlp_shift: bfloat16 [768], P('fsdp'), may hold values from -3 to 3
- weight_up: bfloat16 [768, 3072], P('fsdp'), may hold values from -0.21875 to 0.21875
- bias_up: bfloat16 [3072], P('fsdp'), may hold values from -3 to 3
- weight_down: bfloat16 [3072, 768], P('fsdp'), may hold values from -0.109375 to 0.109375
- bias_down: bfloat16 [768], P('fsdp'), may hold values from -2 to 2
- cotangent: bfloat16 [16, 2048, 768], P('fsdp', 'seq'), may hold values from -6 to 6
Outputs:
- out_rows: bfloat16 [16, 2048, 768], P('fsdp', 'seq')
- grad_input: float32 [16, 2048, 768], P('fsdp', 'seq')
- grad_attn_gain: float32 [768], P('fsdp')
- grad_attn_shift: float32 [768], P('fsdp')
- grad_proj_in: float32 [768, 2304], P('fsdp')
- grad_bias_in: float32 [2304], P('fsdp')
- grad_proj_out: float32 [768, 768], P('fsdp')
- grad_bias_out: float32 [768], P('fsdp')
- grad_mlp_gain: float32 [768], P('fsdp')
- grad_mlp_shift: float32 [768], P('fsdp')
- grad_weight_up: float32 [768, 3072], P('fsdp')
- grad_bias_up: float32 [3072], P('fsdp')
- grad_weight_down: float32 [3072, 768], P('fsdp')
- grad_bias_down: float32 [768], P('fsdp')
Inputs may be any that keep to these rules, and one draw needn't show every extreme that they name: `segment_ids`: along each sequence the ids start at 0, never fall, and end at 15; equal ids mark one document. One document has exactly 512 tokens and begins between 128 and 384; all others are shorter. `block_ids`: A token's block is the number of whole 16-token blocks between its document's first token and it: 0 at a document's first token, rising by one every 16 tokens of the document.
All inputs are finite; a program needn't handle non-finite values.
Results may differ from a plain program's by a relative error of at most 0.015.
Values may be sent and summed in bfloat16 or wider, within the bound.
A program may use at most 104 MiB of HBM per device.

v0:
```python
import jax
import jax.numpy as jnp
from jax import lax
from jax.sharding import PartitionSpec as P

HD = 64


norm_eps = 1e-05


def as_sent(shard):
    return jax.tree.map(lambda a: a.astype(jnp.bfloat16) if a.dtype == jnp.float32 else a, shard)


def row_norm(value, gain, shift):
    center = jnp.mean(value, axis=-1, keepdims=True)
    centered = value - center
    inverse = lax.rsqrt(jnp.mean(centered * centered, axis=-1, keepdims=True) + norm_eps)
    normed = centered * inverse
    return (normed * gain + shift, normed, inverse)


def norm_back(grad, normed, inverse, gain):
    scaled = grad * gain
    first = jnp.mean(scaled, axis=-1, keepdims=True)
    second = jnp.mean(scaled * normed, axis=-1, keepdims=True)
    return (
        inverse * (scaled - first - normed * second),
        jnp.sum(grad * normed, axis=0),
        jnp.sum(grad, axis=0),
    )


def angles(positions, half):
    freqs = 10000.0 ** (-(jnp.arange(half, dtype=jnp.float32) / half))
    turned = positions.astype(jnp.float32)[:, None] * freqs[None, :]
    return (jnp.cos(turned)[:, None, :], jnp.sin(turned)[:, None, :])


def rotate(value, cosine, sine):
    half = value.shape[-1] // 2
    first = value[..., :half]
    second = value[..., half:]
    return jnp.concatenate(
        [first * cosine - second * sine, second * cosine + first * sine], axis=-1
    )


def rotate_back(grad, cosine, sine):
    half = grad.shape[-1] // 2
    first = grad[..., :half]
    second = grad[..., half:]
    return jnp.concatenate(
        [first * cosine + second * sine, second * cosine - first * sine], axis=-1
    )


def allowed(seg_q, blk_q, copy_q, seg_k, blk_k, copy_k):
    same_doc = seg_q[:, None] == seg_k[None, :]
    noisy_q = (copy_q == 0)[:, None]
    noisy_k = (copy_k == 0)[None, :]
    from_noisy = noisy_k & (blk_k[None, :] == blk_q[:, None]) | ~noisy_k & (
        blk_k[None, :] < blk_q[:, None]
    )
    from_clean = ~noisy_k & (blk_k[None, :] <= blk_q[:, None])
    return same_doc & jnp.where(noisy_q, from_noisy, from_clean)


def outer_sum(left, right):
    return lax.dot_general(
        left, right, (((0,), (0,)), ((), ())), preferred_element_type=jnp.float32
    )


def times_transposed(left, weight):
    return lax.dot_general(
        left, weight, (((1,), (1,)), ((), ())), preferred_element_type=jnp.float32
    )


def per_device(
    inputs,
    segment_ids,
    block_ids,
    attn_gain,
    attn_shift,
    proj_in,
    bias_in,
    proj_out,
    bias_out,
    mlp_gain,
    mlp_shift,
    weight_up,
    bias_up,
    weight_down,
    bias_down,
    cotangent,
):
    local = (
        attn_gain,
        attn_shift,
        proj_in,
        bias_in,
        proj_out,
        bias_out,
        mlp_gain,
        mlp_shift,
        weight_up,
        bias_up,
        weight_down,
        bias_down,
    )
    micro, rows, width = inputs.shape
    length = segment_ids.shape[1]
    total = 2 * length
    shard_count = lax.axis_size("fsdp")
    head_dim = HD
    heads_all = width // head_dim
    scale = head_dim ** (-0.5)
    block_rows = min(512, total)
    count = total // block_rows
    sums = tuple((jnp.zeros((p.shape[0] * shard_count,) + p.shape[1:], jnp.float32) for p in local))
    start_row = lax.axis_index("seq") * rows
    positions = (start_row + jnp.arange(rows, dtype=jnp.int32)) % length
    cosine, sine = angles(positions, head_dim // 2)
    copy_all = jnp.arange(total, dtype=jnp.int32) // length
    results = []
    grads_in = []
    for step in range(micro):
        full = (
            lax.all_gather(local[0], "fsdp", axis=0, tiled=True),
            lax.all_gather(local[1], "fsdp", axis=0, tiled=True),
            lax.all_gather(local[2], "fsdp", axis=0, tiled=True),
            lax.all_gather(local[3], "fsdp", axis=0, tiled=True),
            lax.all_gather(local[4], "fsdp", axis=0, tiled=True),
            lax.all_gather(local[5], "fsdp", axis=0, tiled=True),
            lax.all_gather(local[6], "fsdp", axis=0, tiled=True),
            lax.all_gather(local[7], "fsdp", axis=0, tiled=True),
            lax.all_gather(local[8], "fsdp", axis=0, tiled=True),
            lax.all_gather(local[9], "fsdp", axis=0, tiled=True),
            lax.all_gather(local[10], "fsdp", axis=0, tiled=True),
            lax.all_gather(local[11], "fsdp", axis=0, tiled=True),
        )
        (
            gain_one,
            shift_one,
            w_in,
            b_in,
            w_out,
            b_out,
            gain_two,
            shift_two,
            w_up,
            b_up,
            w_down,
            b_down,
        ) = full
        gain_one = gain_one.astype(jnp.float32)
        gain_two = gain_two.astype(jnp.float32)
        rows_f = inputs[step].astype(jnp.float32)
        h_one, n_one, inv_one = row_norm(rows_f, gain_one, shift_one.astype(jnp.float32))
        a_one = h_one.astype(jnp.bfloat16)
        qkv = jnp.dot(a_one, w_in, preferred_element_type=jnp.float32) + b_in.astype(jnp.float32)
        parts = qkv.reshape(rows, 3, heads_all, head_dim)
        q_rot = rotate(parts[:, 0], cosine, sine)
        k_rot = rotate(parts[:, 1], cosine, sine)
        sending = (
            jnp.stack([q_rot, k_rot, parts[:, 2]], axis=1)
            .reshape(rows, 3, width)
            .astype(jnp.bfloat16)
        )
        grouped = lax.all_to_all(sending, "seq", split_axis=2, concat_axis=0, tiled=True)
        local_heads = grouped.shape[2] // head_dim
        q_h = grouped[:, 0].reshape(total, local_heads, head_dim)
        k_h = grouped[:, 1].reshape(total, local_heads, head_dim)
        v_h = grouped[:, 2].reshape(total, local_heads, head_dim)
        seg_all = jnp.concatenate([segment_ids[step], segment_ids[step]])
        blk_all = jnp.concatenate([block_ids[step], block_ids[step]])

        def masked_scores(begin, q_blk):
            mask = allowed(
                lax.dynamic_slice_in_dim(seg_all, begin, block_rows, 0),
                lax.dynamic_slice_in_dim(blk_all, begin, block_rows, 0),
                lax.dynamic_slice_in_dim(copy_all, begin, block_rows, 0),
                seg_all,
                blk_all,
                copy_all,
            )
            scores = (
                jnp.einsum("qhd,khd->hqk", q_blk, k_h, preferred_element_type=jnp.float32) * scale
            )
            return jnp.where(mask[None], scores, -1e30)

        def forward_block(index):
            begin = index * block_rows
            q_blk = lax.dynamic_slice_in_dim(q_h, begin, block_rows, 0)
            scores = masked_scores(begin, q_blk)
            peak = jnp.max(scores, axis=-1, keepdims=True)
            expo = jnp.exp(scores - peak)
            totals = jnp.sum(expo, axis=-1, keepdims=True)
            probs = (expo / totals).astype(jnp.bfloat16)
            attended = jnp.einsum("hqk,khd->qhd", probs, v_h, preferred_element_type=jnp.float32)
            return (attended, peak[..., 0] + jnp.log(totals[..., 0]))

        attended_all, lse_all = lax.map(forward_block, jnp.arange(count, dtype=jnp.int32))
        attn_heads = attended_all.reshape(total, local_heads * head_dim).astype(jnp.bfloat16)
        attn = lax.all_to_all(attn_heads, "seq", split_axis=0, concat_axis=1, tiled=True)
        mid = (
            rows_f
            + jnp.dot(attn, w_out, preferred_element_type=jnp.float32)
            + b_out.astype(jnp.float32)
        )
        h_two, n_two, inv_two = row_norm(mid, gain_two, shift_two.astype(jnp.float32))
        a_two = h_two.astype(jnp.bfloat16)
        upper = jnp.dot(a_two, w_up, preferred_element_type=jnp.float32) + b_up.astype(jnp.float32)
        gated_f, gelu_pull = jax.vjp(lambda value: jax.nn.gelu(value, approximate=True), upper)
        gated = gated_f.astype(jnp.bfloat16)
        final = (
            mid
            + jnp.dot(gated, w_down, preferred_element_type=jnp.float32)
            + b_down.astype(jnp.float32)
        )
        results.append(final.astype(jnp.bfloat16))
        grad_out = cotangent[step]
        grad_out_f = grad_out.astype(jnp.float32)
        g_b_down = jnp.sum(grad_out_f, axis=0)
        g_w_down = outer_sum(gated, grad_out)
        grad_gated = times_transposed(grad_out, w_down)
        grad_upper = gelu_pull(grad_gated)[0].astype(jnp.bfloat16)
        g_b_up = jnp.sum(grad_upper.astype(jnp.float32), axis=0)
        g_w_up = outer_sum(a_two, grad_upper)
        grad_a_two = times_transposed(grad_upper, w_up)
        grad_norm_two, g_gain_two, g_shift_two = norm_back(grad_a_two, n_two, inv_two, gain_two)
        grad_mid = grad_out_f + grad_norm_two
        grad_proj = grad_mid.astype(jnp.bfloat16)
        g_b_out = jnp.sum(grad_proj.astype(jnp.float32), axis=0)
        g_w_out = outer_sum(attn, grad_proj)
        grad_attn = times_transposed(grad_proj, w_out).astype(jnp.bfloat16)
        grad_heads = lax.all_to_all(
            grad_attn, "seq", split_axis=1, concat_axis=0, tiled=True
        ).reshape(total, local_heads, head_dim)

        def backward_block(carry, index):
            grad_keys, grad_values = carry
            begin = index * block_rows
            q_blk = lax.dynamic_slice_in_dim(q_h, begin, block_rows, 0)
            do_blk = lax.dynamic_slice_in_dim(grad_heads, begin, block_rows, 0)
            scores = masked_scores(begin, q_blk)
            probs = jnp.exp(scores - lse_all[index][..., None])
            grad_values = grad_values + jnp.einsum(
                "hqk,qhd->khd",
                probs.astype(jnp.bfloat16),
                do_blk,
                preferred_element_type=jnp.float32,
            )
            grad_probs = jnp.einsum("qhd,khd->hqk", do_blk, v_h, preferred_element_type=jnp.float32)
            inner = jnp.sum(probs * grad_probs, axis=-1, keepdims=True)
            grad_scores = (probs * (grad_probs - inner)).astype(jnp.bfloat16)
            grad_q_blk = (
                jnp.einsum("hqk,khd->qhd", grad_scores, k_h, preferred_element_type=jnp.float32)
                * scale
            )
            grad_keys = (
                grad_keys
                + jnp.einsum("hqk,qhd->khd", grad_scores, q_blk, preferred_element_type=jnp.float32)
                * scale
            )
            return ((grad_keys, grad_values), grad_q_blk)

        empty = jnp.zeros((total, local_heads, head_dim), jnp.float32)
        (grad_keys, grad_values), grad_queries = lax.scan(
            backward_block, (empty, empty), jnp.arange(count, dtype=jnp.int32)
        )
        stacked = jnp.stack(
            [
                grad_queries.reshape(total, local_heads * head_dim),
                grad_keys.reshape(total, local_heads * head_dim),
                grad_values.reshape(total, local_heads * head_dim),
            ],
            axis=1,
        ).astype(jnp.bfloat16)
        back_rows = lax.all_to_all(stacked, "seq", split_axis=0, concat_axis=2, tiled=True).astype(
            jnp.float32
        )
        grad_q_lin = rotate_back(
            back_rows[:, 0].reshape(rows, heads_all, head_dim), cosine, sine
        ).reshape(rows, width)
        grad_k_lin = rotate_back(
            back_rows[:, 1].reshape(rows, heads_all, head_dim), cosine, sine
        ).reshape(rows, width)
        grad_qkv = jnp.concatenate([grad_q_lin, grad_k_lin, back_rows[:, 2]], axis=1).astype(
            jnp.bfloat16
        )
        g_b_in = jnp.sum(grad_qkv.astype(jnp.float32), axis=0)
        g_w_in = outer_sum(a_one, grad_qkv)
        grad_a_one = times_transposed(grad_qkv, w_in)
        grad_norm_one, g_gain_one, g_shift_one = norm_back(grad_a_one, n_one, inv_one, gain_one)
        grads_in.append(grad_mid + grad_norm_one)
        fresh = (
            g_gain_one,
            g_shift_one,
            g_w_in,
            g_b_in,
            g_w_out,
            g_b_out,
            g_gain_two,
            g_shift_two,
            g_w_up,
            g_b_up,
            g_w_down,
            g_b_down,
        )
        sums = tuple((old + new for old, new in zip(sums, fresh)))
    shards = (
        lax.psum_scatter(sums[0], "fsdp", scatter_dimension=0, tiled=True),
        lax.psum_scatter(sums[1], "fsdp", scatter_dimension=0, tiled=True),
        lax.psum_scatter(sums[2], "fsdp", scatter_dimension=0, tiled=True),
        lax.psum_scatter(sums[3], "fsdp", scatter_dimension=0, tiled=True),
        lax.psum_scatter(sums[4], "fsdp", scatter_dimension=0, tiled=True),
        lax.psum_scatter(sums[5], "fsdp", scatter_dimension=0, tiled=True),
        lax.psum_scatter(sums[6], "fsdp", scatter_dimension=0, tiled=True),
        lax.psum_scatter(sums[7], "fsdp", scatter_dimension=0, tiled=True),
        lax.psum_scatter(sums[8], "fsdp", scatter_dimension=0, tiled=True),
        lax.psum_scatter(sums[9], "fsdp", scatter_dimension=0, tiled=True),
        lax.psum_scatter(sums[10], "fsdp", scatter_dimension=0, tiled=True),
        lax.psum_scatter(sums[11], "fsdp", scatter_dimension=0, tiled=True),
    )
    summed = jax.tree.map(lambda part: part.astype(jnp.float32), lax.psum(as_sent(shards), "seq"))
    return (jnp.stack(results), jnp.stack(grads_in)) + tuple(summed)


def solution(mesh):
    return jax.shard_map(
        per_device,
        mesh=mesh,
        in_specs=(
            P("fsdp", "seq", None),
            P("fsdp", None),
            P("fsdp", None),
            P("fsdp"),
            P("fsdp"),
            P("fsdp", None),
            P("fsdp"),
            P("fsdp", None),
            P("fsdp"),
            P("fsdp"),
            P("fsdp"),
            P("fsdp", None),
            P("fsdp"),
            P("fsdp", None),
            P("fsdp"),
            P("fsdp", "seq", None),
        ),
        out_specs=(
            P("fsdp", "seq", None),
            P("fsdp", "seq", None),
            P("fsdp"),
            P("fsdp"),
            P("fsdp", None),
            P("fsdp"),
            P("fsdp", None),
            P("fsdp"),
            P("fsdp"),
            P("fsdp"),
            P("fsdp", None),
            P("fsdp"),
            P("fsdp", None),
            P("fsdp"),
        ),
        check_vma=False,
    )
```

profile of v0, /device:TPU:0, one launch (start us, length us, event | category | flops | bytes accessed | tf_op | source)
XLA Modules:
  0.0 1439.8 jit_solution(18272309918924390158)
XLA Ops:
  17.9 40.3 %all-reduce.16 = (bf16[2304]{0:T(1024)(128)(2,1)S(1)}, bf16[768]{0:T(1024)(128)(2,1)S(1)}, bf16[768]{0:T(1024)(128)(2,1)S(1)}, bf16[768]{0:T(1024)(128)(2,1)S(1)...) all-reduce(bf16[2304]{0:T(1024)(128)(2,1)S(1)} %dynamic-update-slic, ...), channel_id=1, replica_groups=mesh['seq'=4,'fsdp'=8] {'fsdp'}, use_global_device_ids=true, to_apply=%add.2 | all-reduce | flops 6912 | bytes 27648
  61.0 17.6 %all-gather.6.cloned.1.call-done = bf16[768,2304]{1,0:T(8,128)(2,1)} async-done(((bf16[96,2304]{1,0:T(8,128)(2,1)}), bf16[768,2304]{1,0:T(8,128)(2,1)}) %all-gather.6.cloned.1.call-update) | async-done | bytes 3538960 | tf_op jit(solution)/shard_map/all_gather | solution.py:134
  125.8 30.1 %all-to-all-done = bf16[512,3,768]{0,1,2:T(4,128)(2,1)S(1)} async-done(((bf16[512,3,768]{0,1,2:T(4,128)(2,1)}), bf16[512,3,768]{0,1,2:T(4,128)(2,1)S(1)}, u32[]{:S(2)}, u32[]{:S(2)}) %all-to-all-start) | async-done | bytes 2359328 | tf_op jit(solution)/shard_map/all_to_all | solution.py:173
  163.0 26.3 %all-gather = bf16[8,1,384]{2,1,0:T(2,128)(2,1)S(1)} all-gather(bf16[1,1,384]{2,1,0:T(2,128)(2,1)S(1)} %reshape.998), channel_id=1, replica_groups=mesh['seq'=4,'fsdp'=8] {'fsdp'}, dimensions={0}, use_global_device_ids=true | all-gather | bytes 6912 | tf_op jit(solution)/shard_map/all_gather | solution.py:141
  202.5 101.2 %while.59 = (s32[]{:T(128)}, bf16[4,512,3,64]{1,3,2,0:T(8,128)(2,1)}, f32[4,3,512]{2,1,0:T(4,128)S(1)}, s32[4]{0:T(128)S(1)}, s32[2048]{0:T(1024)S(1)}, /*index=...) while((s32[]{:T(128)}, ...), condition=%wide.region_13.14_spmd.clone, body=%wide.region_10.13_spmd.clone.sunk | while | flops 853543936 | bytes 50504984 | solution.py:206
  206.6 6.9 fusion.260
  213.5 6.8 fusion.261
  231.9 6.9 fusion.260
  238.9 6.8 fusion.261
  264.1 6.9 fusion.261
  289.3 6.8 fusion.261
  303.8 15.3 %all-to-all-start.3 = ((bf16[4,512,192]{1,2,0:T(8,128)(2,1)}), bf16[4,512,192]{1,2,0:T(8,128)(2,1)}, u32[]{:S(2)}, u32[]{:S(2)}) async-start(bf16[4,512,192]{1,2,0:T(8,128)(2,1)} %bitcast.385), calls=%async_computation.3 | async-start | bytes 1572864 | tf_op jit(solution)/shard_map/all_to_all | solution.py:208
  320.1 100.8 %while.58 = (s32[]{:T(128)}, bf16[4,512,3,64]{1,3,2,0:T(8,128)(2,1)}, f32[4,3,512]{2,1,0:T(4,128)S(1)}, s32[4]{0:T(128)S(1)}, s32[2048]{0:T(1024)S(1)}, /*index=...) while((s32[]{:T(128)}, ...), condition=%wide.region_5.6_spmd.clone, body=%wide.region_2.5_spmd.clone.sunk | while | flops 853543936 | bytes 50504984 | solution.py:206
  356.0 6.8 fusion.255
  406.4 6.8 fusion.255
  428.6 7.4 all-to-all-done.1
  439.2 7.3 fusion.157
  451.3 11.0 convert_reduce_fusion.1
  462.3 7.2 convert_reduce_fusion
  489.6 8.3 all-to-all-done.6
  504.3 149.7 %while.61 = (s32[]{:T(128)}, f32[2048,3,64]{0,2,1:T(8,128)}, f32[2048,3,64]{0,2,1:T(8,128)}, bf16[4,512,3,64]{1,3,2,0:T(8,128)(2,1)}, s32[4]{0:T(128)S(1)}, /*in...) while((s32[]{:T(128)}, f32[2048,3,64]{0,2,1:T(8,128)}, ...), condition=%wide.region_27.28_spmd.clone.clone, body=%wide.region_25.27_spmd.clone.clone.sunk | while | flops 2073005056 | bytes 147287504 | solution.py:272
  672.3 149.7 %while.60 = (s32[]{:T(128)}, f32[2048,3,64]{0,2,1:T(8,128)}, f32[2048,3,64]{0,2,1:T(8,128)}, bf16[4,512,3,64]{1,3,2,0:T(8,128)(2,1)}, s32[4]{0:T(128)S(1)}, /*in...) while((s32[]{:T(128)}, f32[2048,3,64]{0,2,1:T(8,128)}, ...), condition=%wide.region_20.21_spmd.clone.clone, body=%wide.region_18.20_spmd.clone.clone.sunk | while | flops 2073005056 | bytes 140993936 | solution.py:272
  847.2 37.2 %all-to-all-done.5 = bf16[2048,3,192]{2,1,0:T(4,128)(2,1)} async-done(((bf16[2048,3,192]{2,1,0:T(4,128)(2,1)}), bf16[2048,3,192]{2,1,0:T(4,128)(2,1)}, u32[]{:S(2)}, u32[]{:S(2)}) %all-to-all-start.5) | async-done | bytes 2359328 | tf_op jit(solution)/shard_map/all_to_all | solution.py:283
  884.3 6.9 copy.88
  916.4 10.2 convolution_add_fusion.1
  941.0 8.6 fusion.122
  949.7 8.6 fusion.123
  968.4 36.7 %all-reduce.15 = (bf16[768]{0:T(1024)(128)(2,1)S(1)}, bf16[768]{0:T(1024)(128)(2,1)S(1)}, bf16[2304]{0:T(1024)(128)(2,1)S(1)}, bf16[768]{0:T(1024)(128)(2,1)S(1)...) all-reduce(f32[768]{0:T(1024)S(1)} %add.410, ...), channel_id=2, replica_groups=mesh['seq'=4,'fsdp'=8] {'fsdp'}, use_global_device_ids=true, to_apply=%region_32.33.clone | all-reduce | flops 9984 | bytes 59904
  1017.5 25.8 %reduce-scatter.5.cloned.1.call-done = f32[96,2304]{1,0:T(8,128)} async-done(((f32[768,2304]{1,0:T(8,128)}), f32[96,2304]{1,0:T(8,128)}) %reduce-scatter.5.cloned.1.call-update) | async-done | bytes 884752 | tf_op jit(solution)/shard_map/reduce_scatter | solution.py:318
  1045.2 164.4 %reduce-scatter.11.cloned.1.call-done = f32[384,768]{1,0:T(8,128)} async-done(((f32[3072,768]{1,0:T(8,128)}), f32[384,768]{1,0:T(8,128)}) %reduce-scatter.11.cloned.1.call-update) | async-done | bytes 1179664 | tf_op jit(solution)/shard_map/reduce_scatter | solution.py:326
  1211.8 164.3 %reduce-scatter.9.cloned.1.call-done = f32[96,3072]{1,0:T(8,128)} async-done(((f32[768,3072]{1,0:T(8,128)}), f32[96,3072]{1,0:T(8,128)}) %reduce-scatter.9.cloned.1.call-update) | async-done | bytes 1179664 | tf_op jit(solution)/shard_map/reduce_scatter | solution.py:324
  1383.1 42.7 %all-reduce.21.cloned.1.call-done = (bf16[96,2304]{1,0:T(8,128)(2,1)}, bf16[96,768]{1,0:T(8,128)(2,1)}, bf16[96,3072]{1,0:T(8,128)(2,1)}, bf16[384,768]{1,0:T(8,128)(2,1)}) async-done(((bf16[96,2304]{1,0:T(8,128)(2,1)}, bf16[96,768]{1,0:T(8,128)(2,1)}, bf16[96,3072]{1,0:T(8,128)(2,1)}, bf16[384,768]{1,0:T(8,128)(2,1)}), (bf16[96,2304]{1,0:T(8,128)(2,1)}, bf16[96,768]{1,0:T(8,128)(2,1)}, ...) | async-done | bytes 1769488 | tf_op jit(solution)/shard_map/psum | solution.py:329
  (687 shorter events, 661.9 us)
Async XLA Ops:
  7.2 52.8 %copy-start.14 = (bf16[2,512,768]{2,1,0:T(8,128)(2,1)S(1)}, bf16[2,512,768]{2,1,0:T(8,128)(2,1)}, u32[]{:S(2)}) copy-start(bf16[2,512,768]{2,1,0:T(8,128)(2,1)} %param.24) | copy-start | bytes 4718596
  7.2 71.4 %all-gather.6.cloned.1.call-start = ((), (), s32[]{:S(2)}) async-start(), calls=%async_computation.12 | async-start | bytes 3981312 | tf_op jit(solution)/shard_map/all_gather | solution.py:134
  7.9 416.5 %all-gather.8.cloned.1.call-start = ((), (), s32[]{:S(2)}) async-start(), calls=%async_computation.13 | async-start | bytes 1327104 | tf_op jit(solution)/shard_map/all_gather | solution.py:136
  8.7 430.4 %all-gather.10.cloned.1.call-start = ((), (), s32[]{:S(2)}) async-start(), calls=%async_computation.14 | async-start | bytes 5308416 | tf_op jit(solution)/shard_map/all_gather | solution.py:140
  58.3 32.8 %copy-start.69 = (f32[768]{0:T(1024)}, f32[768]{0:T(1024)S(1)}, u32[]{:S(2)}) copy-start(f32[768]{0:T(1024)S(1)} %convert_element_type.253) | copy-start | bytes 9220
  61.0 47.7 %copy-start.60 = (f32[512,32]{0,1:T(8,128)}, f32[512,32]{0,1:T(8,128)S(1)}, u32[]{:S(2)}) copy-start(f32[512,32]{0,1:T(8,128)S(1)} %get-tuple-element.725) | copy-start | bytes 196612
  61.0 47.7 %copy-start.62 = (f32[512,32]{0,1:T(8,128)}, f32[512,32]{0,1:T(8,128)S(1)}, u32[]{:S(2)}) copy-start(f32[512,32]{0,1:T(8,128)S(1)} %get-tuple-element.726) | copy-start | bytes 196612
  115.0 40.8 %all-to-all-start = ((bf16[512,3,768]{0,1,2:T(4,128)(2,1)}), bf16[512,3,768]{0,1,2:T(4,128)(2,1)S(1)}, u32[]{:S(2)}, u32[]{:S(2)}) async-start(bf16[512,3,768]{0,1,2:T(4,128)(2,1)} %copy.76), calls=%async_computation | async-start | bytes 6291456 | tf_op jit(solution)/shard_map/all_to_all | solution.py:173
  125.8 35.4 %copy-start.107 = (bf16[384]{0:T(512)(128)(2,1)S(1)}, bf16[384]{0:T(512)(128)(2,1)}, u32[]{:S(2)}) copy-start(bf16[384]{0:T(512)(128)(2,1)} %param.36) | copy-start | bytes 2308
  125.8 64.2 %copy-start.99 = (s32[2,1024]{1,0:T(2,128)S(1)}, s32[2,1024]{1,0:T(2,128)}, u32[]{:S(2)}) copy-start(s32[2,1024]{1,0:T(2,128)} %param.26) | copy-start | bytes 24580
  125.8 64.2 %copy-start.100 = (s32[2,1024]{1,0:T(2,128)S(1)}, s32[2,1024]{1,0:T(2,128)}, u32[]{:S(2)}) copy-start(s32[2,1024]{1,0:T(2,128)} %param.25) | copy-start | bytes 24580
  155.9 41.8 %all-to-all-start.2 = ((bf16[512,3,768]{0,1,2:T(4,128)(2,1)}), bf16[512,3,768]{0,1,2:T(4,128)(2,1)}, u32[]{:S(2)}, u32[]{:S(2)}) async-start(bf16[512,3,768]{0,1,2:T(4,128)(2,1)} %copy.80), calls=%async_computation.2 | async-start | bytes 6291456 | tf_op jit(solution)/shard_map/all_to_all | solution.py:173
  160.6 290.6 %all-gather.12.cloned.1.call-start = ((), (), s32[]{:S(2)}) async-start(), calls=%async_computation.15 | async-start | bytes 5308416 | tf_op jit(solution)/shard_map/all_gather | solution.py:142
  303.8 117.1 %all-to-all-start.3 = ((bf16[4,512,192]{1,2,0:T(8,128)(2,1)}), bf16[4,512,192]{1,2,0:T(8,128)(2,1)}, u32[]{:S(2)}, u32[]{:S(2)}) async-start(bf16[4,512,192]{1,2,0:T(8,128)(2,1)} %bitcast.385), calls=%async_computation.3 | async-start | bytes 1572864 | tf_op jit(solution)/shard_map/all_to_all | solution.py:208
  320.0 104.4 %copy-start.105 = (f32[768]{0:T(1024)S(1)}, f32[768]{0:T(1024)}, u32[]{:S(2)}) copy-start(f32[768]{0:T(1024)} %convert_element_type.260) | copy-start | bytes 9220
  420.9 15.1 %all-to-all-start.1 = ((bf16[4,512,192]{1,2,0:T(8,128)(2,1)}), bf16[4,512,192]{1,2,0:T(8,128)(2,1)S(1)}, u32[]{:S(2)}, u32[]{:S(2)}) async-start(bf16[4,512,192]{1,2,0:T(8,128)(2,1)} %bitcast.386), calls=%async_computation.1 | async-start | bytes 1572864 | tf_op jit(solution)/shard_map/all_to_all | solution.py:208
  427.1 49.1 %copy-start.75 = (f32[512]{0:T(512)}, f32[512]{0:T(512)S(1)}, u32[]{:S(2)}) copy-start(f32[512]{0:T(512)S(1)} %broadcast_multiply_fusion.8) | copy-start | bytes 6148
  438.7 33.5 %copy-start.32 = (f32[512,768]{1,0:T(8,128)}, f32[512,768]{1,0:T(8,128)S(1)}, u32[]{:S(2)}) copy-start(f32[512,768]{1,0:T(8,128)S(1)} %get-tuple-element.732) | copy-start | bytes 4718596
  438.7 37.5 %copy-start.83 = (f32[512]{0:T(512)}, f32[512]{0:T(512)S(1)}, u32[]{:S(2)}) copy-start(f32[512]{0:T(512)S(1)} %broadcast_multiply_fusion.10) | copy-start | bytes 6148
  439.1 37.2 %copy-start.79 = (f32[512]{0:T(512)}, f32[512]{0:T(512)S(1)}, u32[]{:S(2)}) copy-start(f32[512]{0:T(512)S(1)} %add_rsqrt_fusion) | copy-start | bytes 6148
  439.1 37.2 %copy-start.97 = (f32[512]{0:T(512)}, f32[512]{0:T(512)S(1)}, u32[]{:S(2)}) copy-start(f32[512]{0:T(512)S(1)} %add_rsqrt_fusion.2) | copy-start | bytes 6148
  482.8 15.1 %all-to-all-start.6 = ((bf16[512,4,192]{0,2,1:T(8,128)(2,1)}), bf16[512,4,192]{0,2,1:T(8,128)(2,1)S(1)}, u32[]{:S(2)}, u32[]{:S(2)}) async-start(bf16[512,4,192]{0,2,1:T(8,128)(2,1)} %bitcast.56), calls=%async_computation.6 | async-start | bytes 1572864 | tf_op jit(solution)/shard_map/all_to_all | solution.py:240
  497.9 158.5 %all-to-all-start.4 = ((bf16[512,4,192]{0,2,1:T(8,128)(2,1)}), bf16[512,4,192]{0,2,1:T(8,128)(2,1)}, u32[]{:S(2)}, u32[]{:S(2)}) async-start(bf16[512,4,192]{0,2,1:T(8,128)(2,1)} %bitcast.40), calls=%async_computation.4 | async-start | bytes 1572864 | tf_op jit(solution)/shard_map/all_to_all | solution.py:240
  666.3 164.8 %all-to-all-start.7 = ((bf16[2048,3,192]{2,1,0:T(4,128)(2,1)}), bf16[2048,3,192]{2,1,0:T(4,128)(2,1)}, u32[]{:S(2)}, u32[]{:S(2)}) async-start(bf16[2048,3,192]{2,1,0:T(4,128)(2,1)} %copy.92), calls=%async_computation.7 | async-start | bytes 8388608 | tf_op jit(solution)/shard_map/all_to_all | solution.py:283
  831.1 53.3 %all-to-all-start.5 = ((bf16[2048,3,192]{2,1,0:T(4,128)(2,1)}), bf16[2048,3,192]{2,1,0:T(4,128)(2,1)}, u32[]{:S(2)}, u32[]{:S(2)}) async-start(bf16[2048,3,192]{2,1,0:T(4,128)(2,1)} %copy.86), calls=%async_computation.5 | async-start | bytes 8388608 | tf_op jit(solution)/shard_map/all_to_all | solution.py:283
  836.1 179.7 %reduce-scatter.7.cloned.1.call-start = ((), (), s32[]{:S(2)}) async-start(), calls=%async_computation.17 | async-start | bytes 2654208 | tf_op jit(solution)/shard_map/reduce_scatter | solution.py:320
  841.6 201.7 %reduce-scatter.5.cloned.1.call-start = ((), (), s32[]{:S(2)}) async-start(), calls=%async_computation.16 | async-start | bytes 7962624 | tf_op jit(solution)/shard_map/reduce_scatter | solution.py:318
  847.2 46.7 %copy-start.25 = (bf16[512,3,4,192]{0,3,2,1:T(8,128)(2,1)}, bf16[512,3,4,192]{0,3,2,1:T(8,128)(2,1)S(1)}, u32[]{:S(2)}) copy-start(bf16[512,3,4,192]{0,3,2,1:T(8,128)(2,1)S(1)} %copy.94) | copy-start | bytes 7077892
  908.9 300.8 %reduce-scatter.11.cloned.1.call-start = ((), (), s32[]{:S(2)}) async-start(), calls=%async_computation.19 | async-start | bytes 10616832 | tf_op jit(solution)/shard_map/reduce_scatter | solution.py:326
  926.6 449.5 %reduce-scatter.9.cloned.1.call-start = ((), (), s32[]{:S(2)}) async-start(), calls=%async_computation.18 | async-start | bytes 10616832 | tf_op jit(solution)/shard_map/reduce_scatter | solution.py:324
  938.6 487.3 %all-reduce.21.cloned.1.call-start = ((), (), s32[]{:S(2)}) async-start(), calls=%async_computation.20 | async-start | bytes 3538944 | tf_op jit(solution)/shard_map/psum | solution.py:329
  1017.5 360.8 %copy-start.22 = (f32[512,768]{1,0:T(8,128)S(1)}, f32[512,768]{1,0:T(8,128)}, u32[]{:S(2)}) copy-start(f32[512,768]{1,0:T(8,128)} %copy-done.20) | copy-start | bytes 4718596
  (137 other events, 823.3 us)
Sparse Core Ops, SparseCore 0:
  10.2 68.3 all-gather.5
  80.8 39.6 all-gather.7
  122.7 78.8 all-gather.9
  203.6 78.0 all-gather.11
  841.7 68.3 reduce-scatter.6
  913.6 129.5 reduce-scatter.4
  1047.3 162.3 reduce-scatter.10
  1213.7 162.4 reduce-scatter.8
  1380.1 45.7 all-reduce.20
where the time goes:
time: 1450 us; the launch traced here: 1440 us
  waiting for transfers between devices  506 us (35%)
  matrix products  425 us (29%)
  other arithmetic  193 us (13%)
  local copies, waits for them, and re-layouts  113 us (8%)
  blocking collectives  109 us (8%)
  starting transfers between devices  45.8 us (3%)
  loops' own time  27.4 us (2%)
  between operations  19.3 us (1%)
    reduce_scatter x1, waiting for transfers between devices, per_device(): lax.psum_scatter(sums[10], 'fsdp', scatter_dimension=0, tiled=True)  164 us
    reduce_scatter x1, waiting for transfers between devices, per_device(): lax.psum_scatter(sums[8], 'fsdp', scatter_dimension=0, tiled=True)  164 us
    dot_general x16, matrix products, masked_scores(): jnp.einsum('qhd,khd->hqk', q_blk, k_h, preferred_element_type=jnp.float32)  78.3 us
    unnamed x2, blocking collectives  77.1 us
    reduce_sum x8, other arithmetic, forward_block(): totals = jnp.sum(expo, axis=-1, keepdims=True)  54.7 us
    dot_general x8, matrix products, forward_block(): jnp.einsum('hqk,khd->qhd', probs, v_h, preferred_element_type=jnp.float32)  53.6 us
    convert_element_type x8, other arithmetic, backward_block(): grad_scores = (probs * (grad_probs - inner)).astype(jnp.bfloat16)  49 us
    dot_general x8, matrix products, backward_block(): jnp.einsum('hqk,qhd->khd', probs.astype(jnp.bfloat16), do_blk, preferred_...  47.4 us
  transfers between devices with their start and end apart: 17, of which 10 were waited for; matrix products, arithmetic and copies ran while one was open for 46% of the time, Pallas kernels for 0%

commit v1 on v0

v1 whole, which is shorter than its diff:
```python
import functools

import jax
import jax.numpy as jnp
from jax import lax
from jax.experimental import pallas as pl
from jax.experimental.pallas import tpu as pltpu
from jax.sharding import PartitionSpec as P

HD = 64
QUAD = 4
TILE = 128
HALO = 16
NEAR = TILE + 2 * HALO
EPS = 1e-05
MASKED = -1e30
SEG_STEP = 4096
F32 = jnp.float32
BF16 = jnp.bfloat16
VMEM_BYTES = 60 * 1024 * 1024


def dot(a, b):
    return jnp.dot(a, b, preferred_element_type=F32)


def dot_nt(a, b):
    return lax.dot_general(a, b, (((1,), (1,)), ((), ())), preferred_element_type=F32)


def dot_tn(a, b):
    return lax.dot_general(a, b, (((0,), (0,)), ((), ())), preferred_element_type=F32)


def norm_stats(x):
    center = jnp.mean(x, axis=-1, keepdims=True)
    centered = x - center
    inverse = lax.rsqrt(jnp.mean(centered * centered, axis=-1, keepdims=True) + EPS)
    return centered * inverse, inverse


def norm_back(grad, normed, inverse, gain):
    scaled = grad * gain
    first = jnp.mean(scaled, axis=-1, keepdims=True)
    second = jnp.mean(scaled * normed, axis=-1, keepdims=True)
    return inverse * (scaled - first - normed * second)


def partner(u):
    lane = lax.broadcasted_iota(jnp.int32, u.shape, 1)
    half = HD // 2
    return jnp.where(
        lane % HD < half, pltpu.roll(u, u.shape[1] - half, 1), pltpu.roll(u, half, 1)
    )


def whole(shape):
    return pl.BlockSpec(shape, lambda *_: (0,) * len(shape), pipeline_mode=pl.Buffered(1))


def call(kernel, grid, in_specs, out_specs, out_shape, scratch, flops, nbytes, name):
    return pl.pallas_call(
        kernel,
        grid=grid,
        in_specs=in_specs,
        out_specs=out_specs,
        out_shape=out_shape,
        scratch_shapes=scratch,
        compiler_params=pltpu.CompilerParams(vmem_limit_bytes=VMEM_BYTES),
        cost_estimate=pl.CostEstimate(flops=flops, bytes_accessed=nbytes, transcendentals=0),
        name=name,
    )


def like(shape, dtype):
    return jax.ShapeDtypeStruct(shape, dtype)


SMEM = functools.partial(pl.BlockSpec, memory_space=pltpu.SMEM)


def layout(rows, length):
    win = rows - length // 8
    noisy = win + rows + HALO
    return dict(rows=rows, win=win, length=length, noisy=noisy, keys=noisy + rows + 2 * HALO)


def places(lay, role):
    noisy = role[0] == 0
    second = role[1] == 1
    own_at = jnp.where(noisy, lay["noisy"] + HALO, lay["win"])
    halo_at = jnp.where(
        second,
        lay["noisy"],
        jnp.where(noisy, lay["noisy"] + HALO + lay["rows"], lay["win"] + lay["rows"]),
    )
    return noisy, second, pl.multiple_of(own_at, HALO), pl.multiple_of(halo_at, HALO)


def qkv_kernel(lay, role, x, xb, xc, w, b, gain, shift, cos, sin, q_out, k_out, v_out, a_out):
    width = x.shape[2]
    rows, win = lay["rows"], lay["win"]
    noisy, second, own_at, halo_at = places(lay, role)

    def norm(v):
        normed, _ = norm_stats(v.astype(F32))
        return (normed * gain[...] + shift[...]).astype(BF16)

    def zeros(at, count):
        k_out[0, at : at + count, :] = jnp.zeros((count, width), BF16)
        v_out[0, at : at + count, :] = jnp.zeros((count, width), BF16)

    def section(a, parts, table, want_q):
        def put(ref, col, value):
            for begin, count, at in parts:
                ref[0, pl.ds(at, count), col : col + value.shape[1]] = value[begin : begin + count]

        put(a_out, 0, a)
        c = cos[table : table + a.shape[0], :]
        s = sin[table : table + a.shape[0], :]
        first = 0 if want_q else width
        for col in range(first, 3 * width, 256):
            part = dot(a, w[:, col : col + 256]) + b[:, col : col + 256]
            for piece in range(2):
                u = part[:, piece * 128 : piece * 128 + 128]
                at_col = col + piece * 128
                if at_col < 2 * width:
                    u = u * c + partner(u) * s
                if at_col < width:
                    q_out[0, :, at_col : at_col + 128] = (u[:rows] * (HD**-0.5)).astype(BF16)
                elif at_col < 2 * width:
                    put(k_out, at_col - width, u.astype(BF16))
                else:
                    put(v_out, at_col - 2 * width, u.astype(BF16))

    zeros(win + rows, 2 * HALO)
    zeros(lay["keys"] - HALO, HALO)
    own = jnp.concatenate([norm(x[0]), norm(xc[0, win:, :])], axis=0)
    section(own, ((0, rows, own_at), (rows, HALO, halo_at)), win, True)

    @pl.when(noisy)
    def _():
        section(norm(xb[0]), ((0, rows, win),), win, False)

    @pl.when(jnp.logical_not(noisy))
    def _():
        zeros(lay["noisy"] + HALO, rows)

    @pl.when(second)
    def _():
        section(norm(xc[0, :win, :]), ((0, win, 0),), 0, False)

    @pl.when(jnp.logical_not(second))
    def _():
        zeros(0, win)


def windows(lay):
    rows, win, length = lay["rows"], lay["win"], lay["length"]
    longest, earliest, latest = length // 2, length // 8, 3 * length // 8
    found = []
    for at in range(0, rows, TILE):
        begin = win + rows
        for origin in range(0, length, rows):
            pos = origin + at
            low = max(pos - longest, 0)
            if origin > 0:
                low = max(low, earliest)
            if pos >= latest + longest:
                low = max(low, earliest + longest)
            begin = min(begin, low - origin + win)
        found.append((begin // TILE * TILE, win + at + TILE + HALO))
    return found


def make_bias(lay, codes, queries, biases):
    for t, (lo, hi) in enumerate(windows(lay)):
        here = slice(t * TILE, t * TILE + TILE)
        low, high, same = (queries[0, n : n + 1, here] for n in range(3))
        kc = codes[0, lo:hi, :]
        ok = (kc >= low) & (kc <= high)
        biases[t][: hi - lo, :] = jnp.where(ok, 0.0, MASKED)
        near = lay["noisy"] + t * TILE
        kn = codes[0, near : near + NEAR, :]
        biases[t][hi - lo :, :] = jnp.where(kn == same, 0.0, MASKED)


def stacked(tile):
    lane = lax.broadcasted_iota(jnp.int32, tile.shape, 1)
    zero = jnp.zeros_like(tile)
    return jnp.concatenate(
        [jnp.where(lane // HD == h, tile, zero) for h in range(QUAD)], axis=0
    )


def own_heads(wide):
    return jnp.concatenate(
        [wide[h * HD : h * HD + HD, h * TILE : h * TILE + TILE] for h in range(QUAD)], axis=0
    )


def keys_of(ref, lay, t, lo, hi):
    near = lay["noisy"] + t * TILE
    return jnp.concatenate([ref[0, lo:hi, :], ref[0, near : near + NEAR, :]], axis=0)


def attend_kernel(lay, codes, queries, q, k, v, o_out, lse_out, *biases):
    @pl.when(pl.program_id(1) == 0)
    def _():
        make_bias(lay, codes, queries, biases)

    for t, (lo, hi) in enumerate(windows(lay)):
        qm = stacked(q[0, t * TILE : t * TILE + TILE, :])
        kk = keys_of(k, lay, t, lo, hi)
        vv = keys_of(v, lay, t, lo, hi)
        s = dot_nt(kk, qm) + jnp.concatenate([biases[t][...]] * QUAD, axis=1)
        peak = jnp.max(s, axis=0, keepdims=True)
        p = jnp.exp(s - peak)
        total = jnp.sum(p, axis=0, keepdims=True)
        wide = dot_tn(vv, p.astype(BF16)) * (1.0 / total)
        o_out[0, t * TILE : t * TILE + TILE, :] = jnp.transpose(own_heads(wide)).astype(BF16)
        lse_out[0, 0, t : t + 1, :] = peak + jnp.log(total)


def attend_back_kernel(
    lay, codes, queries, q, k, v, o, do, lse, cos, sin, dq_out, dk_out, dv_out, dk_acc, dv_acc, *biases
):
    rows, win = lay["rows"], lay["win"]

    @pl.when(pl.program_id(1) == 0)
    def _():
        make_bias(lay, codes, queries, biases)

    dk_acc[...] = jnp.zeros_like(dk_acc)
    dv_acc[...] = jnp.zeros_like(dv_acc)
    for t, (lo, hi) in enumerate(windows(lay)):
        here = slice(t * TILE, t * TILE + TILE)
        size = hi - lo
        near = slice(lay["noisy"] + t * TILE, lay["noisy"] + t * TILE + NEAR)
        qm = stacked(q[0, here, :])
        dom = stacked(do[0, here, :])
        kk = keys_of(k, lay, t, lo, hi)
        vv = keys_of(v, lay, t, lo, hi)
        both = jnp.transpose(do[0, here, :].astype(F32) * o[0, here, :].astype(F32))
        delta = jnp.concatenate(
            [jnp.sum(both[h * HD : h * HD + HD, :], axis=0, keepdims=True) for h in range(QUAD)],
            axis=1,
        )
        s = dot_nt(kk, qm) + jnp.concatenate([biases[t][...]] * QUAD, axis=1)
        p = jnp.exp(s - lse[0, 0, t : t + 1, :])
        dp = dot_nt(vv, dom)
        ds = (p * (dp - delta)).astype(BF16)
        pb = p.astype(BF16)
        dv = dot(pb, dom)
        dk = dot(ds, qm)
        dv_acc[lo:hi, :] += dv[:size]
        dk_acc[lo:hi, :] += dk[:size]
        dv_acc[near, :] += dv[size:]
        dk_acc[near, :] += dk[size:]
        wide = dot_tn(kk, ds)
        dq = jnp.transpose(own_heads(wide)) * (HD**-0.5)
        c = cos[win + t * TILE : win + t * TILE + TILE, :]
        sn = sin[win + t * TILE : win + t * TILE + TILE, :]
        for piece in range(2):
            u = dq[:, piece * 128 : piece * 128 + 128]
            dq_out[0, here, piece * 128 : piece * 128 + 128] = (u * c - partner(u) * sn).astype(BF16)
    dv_out[0] = dv_acc[...].astype(BF16)
    half = (cos[win + rows :, :], sin[win + rows :, :])
    own = (cos[win : win + rows, :], sin[win : win + rows, :])
    tables = (
        (0, (cos[: win + rows, :], sin[: win + rows, :])),
        (win + rows, half),
        (lay["noisy"], half),
        (lay["noisy"] + HALO, own),
        (lay["keys"] - HALO, half),
    )
    for at, (c, sn) in tables:
        here = slice(at, at + c.shape[0])
        for piece in range(2):
            cols = slice(piece * 128, piece * 128 + 128)
            u = dk_acc[here, cols]
            dk_out[0, here, cols] = (u * c - partner(u) * sn).astype(BF16)


def mlp_kernel(
    o, x, dy, w_out, b_out, gain, shift, w_up, b_up, w_down, b_down,
    out_rows, dx2_out, do_out, g_w_out, g_w_up, g_b_up, g_w_down, g_vec,
    mid, a2, a2t, inv, acc_out, acc_da,
):
    step = pl.program_id(0)
    last = pl.num_programs(0) - 1

    @pl.when(step == 0)
    def _():
        value = x[...].astype(F32) + dot(o[...], w_out[...]) + b_out[...]
        mid[...] = value
        normed, inverse = norm_stats(value)
        inv[...] = inverse
        a = (normed * gain[...] + shift[...]).astype(BF16)
        a2[...] = a
        a2t[...] = jnp.transpose(a)
        acc_out[...] = jnp.zeros_like(acc_out)
        acc_da[...] = jnp.zeros_like(acc_da)

    u = dot(a2[...], w_up[...]) + b_up[...]
    scale = 0.7978845608028654
    square = u * u
    inner = scale * u * (1.0 + 0.044715 * square)
    th = jnp.tanh(inner)
    plus = 0.5 * (1.0 + th)
    g = (u * plus).astype(BF16)
    slope = plus + 0.5 * u * (1.0 - th * th) * (scale * (1.0 + 3 * 0.044715 * square))
    acc_out[...] += dot(g, w_down[...])
    du32 = dot_nt(dy[...], w_down[...]) * slope
    du = du32.astype(BF16)
    g_b_up[...] = jnp.broadcast_to(jnp.sum(du.astype(F32), axis=0, keepdims=True), g_b_up.shape)
    acc_da[...] += dot_nt(du, w_up[...])
    g_w_down[...] = dot_tn(g, dy[...]).astype(BF16)
    g_w_up[...] = dot(a2t[...], du).astype(BF16)

    @pl.when(step == last)
    def _():
        dyf = dy[...].astype(F32)
        out_rows[...] = (mid[...] + acc_out[...] + b_down[...]).astype(BF16)
        inverse = inv[...]
        value = mid[...]
        normed = (value - jnp.mean(value, axis=-1, keepdims=True)) * inverse
        da = acc_da[...]
        dx2 = dyf + norm_back(da, normed, inverse, gain[...])
        dx2_out[...] = dx2
        dp = dx2.astype(BF16)
        do_out[...] = dot_nt(dp, w_out[...]).astype(BF16)
        g_w_out[...] = dot_tn(o[...], dp).astype(BF16)
        g_vec[...] = jnp.concatenate(
            [
                jnp.sum(dyf, axis=0, keepdims=True),
                jnp.sum(da * normed, axis=0, keepdims=True),
                jnp.sum(da, axis=0, keepdims=True),
                jnp.sum(dp.astype(F32), axis=0, keepdims=True),
                jnp.zeros((4, dyf.shape[1]), F32),
            ],
            axis=0,
        )


def qkv_back_kernel(lay, role, a, dq, dk, dv, w, da_own, da_main, da_win, g_w, g_b, g_acc):
    width = dq.shape[2]
    rows, win = lay["rows"], lay["win"]
    noisy, second, own_at, halo_at = places(lay, role)

    @pl.when(pl.program_id(0) == 0)
    def _():
        g_acc[...] = jnp.zeros_like(g_acc)
        g_b[...] = jnp.zeros_like(g_b)

    def column_sums(col, value):
        g_b[0:1, col : col + width] += jnp.sum(value.astype(F32), axis=0, keepdims=True)

    def section(parts, query):
        def take(ref):
            return jnp.concatenate([ref[0, pl.ds(at, count), :] for at, count in parts], axis=0)

        at_t = jnp.transpose(take(a))
        key = take(dk)
        value = take(dv)
        g_acc[:, width : 2 * width] += dot(at_t, key)
        g_acc[:, 2 * width :] += dot(at_t, value)
        column_sums(width, key)
        column_sums(2 * width, value)
        total = dot_nt(key, w[:, width : 2 * width]) + dot_nt(value, w[:, 2 * width :])
        if query is not None:
            g_acc[:, :width] += dot(at_t[:, : query.shape[0]], query)
            column_sums(0, query)
            first = total[: query.shape[0]] + dot_nt(query, w[:, :width])
            return first, total[query.shape[0] :]
        return total

    own, near = section(((own_at, rows), (halo_at, HALO)), dq[0])
    da_own[0] = own
    da_win[0, win:, :] = near.astype(BF16)

    @pl.when(noisy)
    def _():
        da_main[0] = section(((win, rows),), None).astype(BF16)

    @pl.when(second)
    def _():
        da_win[0, :win, :] = section(((0, win),), None).astype(BF16)

    @pl.when(pl.program_id(0) == pl.num_programs(0) - 1)
    def _():
        g_w[...] = g_acc[...].astype(BF16)


def final_kernel(x, da, extra, dx2, gain, grad_in, g_vec):
    value = x[...].astype(F32)
    normed, inverse = norm_stats(value)
    grad = da[...] + extra[...].astype(F32)
    grad_in[...] = dx2[...] + norm_back(grad, normed, inverse, gain[...])

    @pl.when(pl.program_id(0) == 0)
    def _():
        g_vec[...] = jnp.zeros_like(g_vec)

    g_vec[0:1, :] += jnp.sum(grad * normed, axis=0, keepdims=True)
    g_vec[1:2, :] += jnp.sum(grad, axis=0, keepdims=True)


def per_device(
    inputs, segment_ids, block_ids, attn_gain, attn_shift, proj_in, bias_in, proj_out, bias_out,
    mlp_gain, mlp_shift, weight_up, bias_up, weight_down, bias_down, cotangent,
):
    micro, rows, width = inputs.shape
    length = segment_ids.shape[1]
    hidden = weight_up.shape[1]
    seq_n = lax.axis_size("seq")
    fsdp_n = lax.axis_size("fsdp")
    assert seq_n == 4 and seq_n * rows == 2 * length
    lay = layout(rows, length)
    win, keys = lay["win"], lay["keys"]
    me = lax.axis_index("seq")
    clean = me // 2
    half = me % 2
    role = jnp.stack([clean, half]).astype(jnp.int32)
    pairs = [(0, 1), (1, 0), (2, 3), (3, 2)]

    xb = lax.ppermute(inputs, "seq", [(2, 0), (3, 1)])
    xmain = jnp.where(clean == 1, inputs, xb)
    edge = jnp.where(half == 0, inputs[:, rows - HALO :], inputs[:, :HALO])
    xc = lax.ppermute(jnp.concatenate([xmain[:, rows - win :], edge], axis=1), "seq", pairs)

    start = half * rows
    edge_at = jnp.where(half == 0, rows, -HALO)
    positions = start + jnp.concatenate([jnp.arange(-win, rows), edge_at + jnp.arange(HALO)])
    freqs = 10000.0 ** (-(jnp.arange(HD // 2, dtype=F32) / (HD // 2)))
    turned = positions.astype(F32)[:, None] * freqs[None, :]
    cosine, sine = jnp.cos(turned), jnp.sin(turned)
    cos = jnp.concatenate([cosine] * 4, axis=1)
    sin = jnp.concatenate([-sine, sine] * 2, axis=1)

    code = segment_ids * SEG_STEP + block_ids
    padded = jnp.pad(code, ((0, 0), (win, 0)), constant_values=-1)
    key_codes = lax.dynamic_slice_in_dim(padded, start, win + rows, 1)
    own_code = lax.dynamic_slice_in_dim(code, start, rows, 1)
    own_seg = lax.dynamic_slice_in_dim(segment_ids, start, rows, 1)
    before, after = code[:, rows - HALO : rows], code[:, rows : rows + HALO]
    codes = jnp.concatenate(
        [
            key_codes,
            jnp.where((clean == 1) & (half == 0), after, -1),
            jnp.where((clean == 0) & (half == 1), before, -2),
            jnp.where(clean == 0, own_code, -2),
            jnp.where((clean == 0) & (half == 0), after, -2),
        ],
        axis=1,
    )[:, :, None]
    queries = jnp.stack([own_seg * SEG_STEP, own_code - (1 - clean), own_code], axis=1)
    queries = jnp.concatenate([queries, jnp.zeros((micro, 5, rows), jnp.int32)], axis=1)

    small = (attn_gain, attn_shift, bias_in, bias_out, mlp_gain, mlp_shift, bias_up, bias_down)
    sizes = [p.shape[0] for p in small]
    packed = lax.all_gather(jnp.concatenate(small)[None], "fsdp", axis=0, tiled=True)
    vectors, at = [], 0
    for size in sizes:
        vectors.append(packed[:, at : at + size].reshape(1, -1).astype(F32))
        at += size
    gain1, shift1, b_in, b_out, gain2, shift2, b_up, b_down = vectors
    w_in, w_out, w_up, w_down = (
        lax.all_gather(p, "fsdp", axis=0, tiled=True)
        for p in (proj_in, proj_out, weight_up, weight_down)
    )

    quads = width // (QUAD * HD)
    qw = QUAD * HD
    spans = [hi - lo + NEAR for lo, hi in windows(lay)]
    bias_scratch = [pltpu.VMEM((n, TILE), F32) for n in spans]
    per_seq = lambda n, d: pl.BlockSpec((1, n, d), lambda s: (s, 0, 0))
    role_spec = SMEM()

    q, k, v, a = call(
        functools.partial(qkv_kernel, lay), (micro,),
        [role_spec, per_seq(rows, width), per_seq(rows, width), per_seq(win + HALO, width),
         whole((width, 3 * width)), whole((1, 3 * width)), whole((1, width)), whole((1, width)),
         whole((win + rows + HALO, 128)), whole((win + rows + HALO, 128))],
        [per_seq(rows, width), per_seq(keys, width), per_seq(keys, width), per_seq(keys, width)],
        [like((micro, rows, width), BF16)] + [like((micro, keys, width), BF16)] * 3,
        [], 2 * micro * rows * width * 3 * width * 2, 20 << 20, "qkv",
    )(role, inputs, xb, xc, w_in, b_in, gain1, shift1, cos, sin)

    quad_block = lambda n: pl.BlockSpec((1, n, qw), lambda s, h: (s, 0, h))
    code_spec = pl.BlockSpec((1, keys, 1), lambda s, h: (s, 0, 0))
    query_spec = pl.BlockSpec((1, 8, rows), lambda s, h: (s, 0, 0))
    lse_spec = pl.BlockSpec((1, 1, rows // TILE, QUAD * TILE), lambda s, h: (s, h, 0, 0))
    attn_flops = micro * quads * sum(spans) * QUAD * TILE * qw * 2
    o, lse = call(
        functools.partial(attend_kernel, lay), (micro, quads),
        [code_spec, query_spec, quad_block(rows), quad_block(keys), quad_block(keys)],
        [quad_block(rows), lse_spec],
        [like((micro, rows, width), BF16), like((micro, quads, rows // TILE, QUAD * TILE), F32)],
        bias_scratch, 2 * attn_flops, 12 << 20, "attend",
    )(codes, queries, q, k, v)

    total = micro * rows
    flat = lambda z: z.reshape(total, width)
    chunk = min(512, hidden)
    vec = whole((1, width))
    rows_spec = whole((total, width))
    out_rows, dx2, do, g_w_out, g_w_up, g_b_up, g_w_down, g_mlp = call(
        mlp_kernel, (hidden // chunk,),
        [rows_spec, rows_spec, rows_spec, whole((width, width)), vec, vec, vec,
         pl.BlockSpec((width, chunk), lambda j: (0, j)), pl.BlockSpec((1, chunk), lambda j: (0, j)),
         pl.BlockSpec((chunk, width), lambda j: (j, 0)), vec],
        [rows_spec, rows_spec, rows_spec, whole((width, width)),
         pl.BlockSpec((width, chunk), lambda j: (0, j)), pl.BlockSpec((8, chunk), lambda j: (0, j)),
         pl.BlockSpec((chunk, width), lambda j: (j, 0)), whole((8, width))],
        [like((total, width), BF16), like((total, width), F32), like((total, width), BF16),
         like((width, width), BF16), like((width, hidden), BF16), like((8, hidden), F32),
         like((hidden, width), BF16), like((8, width), F32)],
        [pltpu.VMEM((total, width), F32), pltpu.VMEM((total, width), BF16), pltpu.VMEM((width, total), BF16),
         pltpu.VMEM((total, 1), F32), pltpu.VMEM((total, width), F32), pltpu.VMEM((total, width), F32)],
        2 * total * width * (6 * hidden + 3 * width), 40 << 20, "mlp",
    )(flat(o), flat(inputs), flat(cotangent), w_out, b_out, gain2, shift2, w_up, b_up, w_down, b_down)

    seqs = lambda z: z.reshape(micro, rows, width)
    table = pl.BlockSpec((win + rows + HALO, 128), lambda s, h: (0, 0), pipeline_mode=pl.Buffered(1))
    dq, dk, dv = call(
        functools.partial(attend_back_kernel, lay), (micro, quads),
        [code_spec, query_spec, quad_block(rows), quad_block(keys), quad_block(keys),
         quad_block(rows), quad_block(rows), lse_spec, table, table],
        [quad_block(rows), quad_block(keys), quad_block(keys)],
        [like((micro, rows, width), BF16), like((micro, keys, width), BF16), like((micro, keys, width), BF16)],
        [pltpu.VMEM((keys, qw), F32), pltpu.VMEM((keys, qw), F32)] + bias_scratch,
        5 * attn_flops, 24 << 20, "attend_back",
    )(codes, queries, q, k, v, o, seqs(do), lse, cos, sin)

    da_own, da_main, da_win, g_w_in, g_b_in = call(
        functools.partial(qkv_back_kernel, lay), (micro,),
        [role_spec, per_seq(keys, width), per_seq(rows, width), per_seq(keys, width), per_seq(keys, width),
         whole((width, 3 * width))],
        [per_seq(rows, width), per_seq(rows, width), per_seq(win + HALO, width),
         whole((width, 3 * width)), whole((8, 3 * width))],
        [like((micro, rows, width), F32), like((micro, rows, width), BF16), like((micro, win + HALO, width), BF16),
         like((width, 3 * width), BF16), like((8, 3 * width), F32)],
        [pltpu.VMEM((width, 3 * width), F32)], 2 * 2 * micro * rows * width * 3 * width * 2, 40 << 20, "qkv_back",
    )(role, a, dq, dk, dv, w_in)

    from_pair = lax.ppermute(da_win, "seq", pairs).astype(F32)
    from_second = jnp.where(half == 0, from_pair[:, :win], 0.0)
    edge = from_pair[:, win:]
    gap = jnp.zeros((micro, rows - HALO, width), F32)
    edges = jnp.where(
        half == 0, jnp.concatenate([gap, edge], axis=1), jnp.concatenate([edge, gap], axis=1)
    )
    added = jnp.pad(from_second, ((0, 0), (rows - win, 0), (0, 0)))
    to_clean = (jnp.where(clean == 0, da_main.astype(F32), 0.0) + added).astype(BF16)
    from_noisy = lax.ppermute(to_clean, "seq", [(0, 2), (1, 3)])
    extra = jnp.where(clean == 1, from_noisy.astype(F32) + added, 0.0) + edges

    grad_in, g_attn = call(
        final_kernel, (2,),
        [pl.BlockSpec((total // 2, width), lambda i: (i, 0))] * 4 + [vec],
        [pl.BlockSpec((total // 2, width), lambda i: (i, 0)), whole((8, width))],
        [like((total, width), F32), like((8, width), F32)], [], 0, 16 << 20, "norm_back",
    )(flat(inputs), flat(da_own), flat(extra), dx2, gain1)

    def scatter(g):
        return lax.psum(lax.psum_scatter(g, "fsdp", scatter_dimension=0, tiled=True), "seq")

    big = [scatter(g).astype(F32) for g in (g_w_in, g_w_out, g_w_up, g_w_down)]
    smalls = [g_attn[0], g_attn[1], g_b_in[0], g_mlp[3], g_mlp[1], g_mlp[2], g_b_up[0], g_mlp[0]]
    pack = jnp.concatenate([g.reshape(fsdp_n, -1) for g in smalls], axis=1)
    pack = lax.psum(pack, ("seq", "fsdp"))
    mine = lax.dynamic_slice_in_dim(pack, lax.axis_index("fsdp"), 1, 0)[0]
    outs, at = [], 0
    for size in sizes:
        outs.append(mine[at : at + size])
        at += size
    g_gain1, g_shift1, g_bin, g_bout, g_gain2, g_shift2, g_bup, g_bdown = outs
    return (
        seqs(out_rows), seqs(grad_in), g_gain1, g_shift1, big[0], g_bin, big[1], g_bout,
        g_gain2, g_shift2, big[2], g_bup, big[3], g_bdown,
    )


def solution(mesh):
    rows = P("fsdp", "seq", None)
    one, two = P("fsdp"), P("fsdp", None)
    params = (one, one, two, one, two, one, one, one, two, one, two, one)
    return jax.shard_map(
        per_device,
        mesh=mesh,
        in_specs=(rows, two, two) + params + (rows,),
        out_specs=(rows, rows) + params,
        check_vma=False,
    )
```

time: 1450 us -> 756 us (0.52)
  matrix products: 425 us -> 0 us
  other arithmetic: 193 us -> 18.1 us
  Pallas kernels: 0 us -> 162 us
  local copies, waits for them, and re-layouts: 113 us -> 24 us
  waiting for transfers between devices: 506 us -> 446 us
  starting transfers between devices: 45.8 us -> 7.58 us
  blocking collectives: 109 us -> 80.5 us
  loops' own time: 27.4 us -> 0 us
    dot_general x80 -> x0, matrix products: 425 us -> none  [the longest x16 78.3 us: masked_scores(): jnp.einsum('qhd,khd->hqk', q_blk, k_h, preferred_element_type=jnp.float32)]
    pallas_call x0 -> x6, Pallas kernels: none -> 162 us  [the longest x1 59.9 us: per_device(): call(mlp_kernel, (hidden // chunk,), [rows_spec, rows_spec, rows_spec, wh...]
    all_gather x4, waiting for transfers between devices: 17.7 us -> 168 us  [per_device(): lax.all_gather(p, 'fsdp', axis=0, tiled=True)]
    all_to_all x8 -> x0, waiting for transfers between devices: 88.6 us -> none  [the longest x2 37.2 us: per_device(): lax.all_to_all(stacked, 'seq', split_axis=0, concat_axis=2, tiled=True)]
    reduce_scatter x4, waiting for transfers between devices: 355 us -> 271 us  [scatter(): lax.psum_scatter(g, 'fsdp', scatter_dimension=0, tiled=True)]
    convert_element_type x35 -> x9, other arithmetic: 73.7 us -> 7.96 us  [the longest x4 6.1 us: per_device(): big = [scatter(g).astype(F32) for g in (g_w_in, g_w_out, g_w_up, g_w_down)]]
    reduce_sum x15 -> x0, other arithmetic: 61.7 us -> none  [the longest x8 54.7 us: forward_block(): totals = jnp.sum(expo, axis=-1, keepdims=True)]
    all_to_all x8 -> x0, starting transfers between devices: 45.2 us -> none  [the longest x2 18.8 us: per_device(): lax.all_to_all(attn_heads, 'seq', split_axis=0, concat_axis=1, tiled=True)]
  transfers between devices with their start and end apart: 17 -> 13, of which waited for: 10 -> 8; matrix products, arithmetic and copies ran while one was open for 46% -> 4% of each run, Pallas kernels for 0% -> 14%
where the time goes in v1:
time: 756 us; the launch traced here: 753 us
  waiting for transfers between devices  446 us (59%)
  Pallas kernels  162 us (21%)
  blocking collectives  80.5 us (11%)
  local copies, waits for them, and re-layouts  24 us (3%)
  other arithmetic  18.1 us (2%)
  between operations  15 us (2%)
  starting transfers between devices  7.58 us (1%)
    reduce_scatter x4, waiting for transfers between devices, scatter(): lax.psum_scatter(g, 'fsdp', scatter_dimension=0, tiled=True)  271 us
    all_gather x4, waiting for transfers between devices, per_device(): lax.all_gather(p, 'fsdp', axis=0, tiled=True)  168 us
    pallas_call x1, Pallas kernels, per_device(): call(mlp_kernel, (hidden // chunk,), [rows_spec, rows_spec, rows_spec, wh...  59.9 us
    psum x1, blocking collectives, per_device(): pack = lax.psum(pack, ('seq', 'fsdp'))  40.8 us
    unnamed x1, blocking collectives  39.7 us
    pallas_call x1, Pallas kernels, per_device(): call(functools.partial(attend_back_kernel, lay), (micro, quads), [code_sp...  33.2 us
    pallas_call x1, Pallas kernels, per_device(): call(functools.partial(attend_kernel, lay), (micro, quads), [code_spec, q...  24.7 us
    pallas_call x1, Pallas kernels, per_device(): call(functools.partial(qkv_back_kernel, lay), (micro,), [role_spec, per_s...  22.7 us
  transfers between devices with their start and end apart: 13, of which 8 were waited for; matrix products, arithmetic and copies ran while one was open for 4% of the time, Pallas kernels for 14%

profile of v1, /device:TPU:0, one launch (start us, length us, event | category | flops | bytes accessed | tf_op | source)
XLA Modules:
  0.0 753.1 jit_solution(14220934544756088395)
XLA Ops:
  10.0 1.3 collective-permute-start
  11.4 1.2 dynamic-slice
  13.3 5.5 concatenate.37
  19.0 39.7 %all-reduce.4 = bf16[9984]{0:T(1024)(128)(2,1)S(1)} all-reduce(bf16[9984]{0:T(1024)(128)(2,1)S(1)} %dynamic-update-slice), channel_id=2, replica_groups=mesh['seq'=4,'fsdp'=8] {'fsdp'}, use_global_device_ids=true, to_apply=%add.4 | all-reduce | flops 9984 | bytes 39936
  64.0 1.6 copy.33.codes
  69.5 1.7 fusion.3
  71.2 1.7 pad_maximum_fusion.1
  73.6 5.0 all-gather.6.cloned.1.call-done.w
  78.6 15.0 %qkv.1 = (bf16[2,512,768]{2,1,0:T(8,128)(2,1)}, bf16[2,1456,768]{2,1,0:T(8,128)(2,1)}, bf16[2,1456,768]{2,1,0:T(8,128)(2,1)}, bf16[2,1456,768]{2,1,0:T(8,128)(2,1)}) custom-call(s32[2]{0:T(128)} %pad_add_fusion.2.role, bf16[2,512,768]{2,1,0:T(8,128)(2,1)} %x.10, bf16[2,512,768]{2,1,0:T(8,128)(2,1)} %copy-done.3, ...), custom_call_target="tpu_custom_call" | custom-call | flops 7247757312 | bytes 20971520 | tf_op jit(solution)/shard_map/qkv/pallas_call | solution.py:480
  93.6 24.7 %attend.1 = (bf16[2,512,768]{2,1,0:T(8,128)(2,1)}, f32[2,3,4,512]{3,2,1,0:T(4,128)}) custom-call(s32[2,1456,1]{2,1,0:T(8,128)} %copy.33.codes, s32[2,8,512]{2,1,0:T(8,128)} %add_add_fusion.queries, bf16[2,512,768]{2,1,0:T(8,128)(2,1)} %get-tuple-element.38.q, bf16[2,1456,768]{2,1,0:T(8,128)(2,1)} %get-tuple-element.39.k, ...), custom_call_target="tpu_custom_call" | custom-call | flops 9462349824 | bytes 12582912 | tf_op jit(solution)/shard_map/attend/pallas_call | solution.py:495
  118.2 2.3 all-gather.8.cloned.1.call-done.w_out
  120.6 80.9 %all-gather.10.cloned.1.call-done.w_up = bf16[768,3072]{1,0:T(8,128)(2,1)} async-done(((bf16[96,3072]{1,0:T(8,128)(2,1)}), bf16[768,3072]{1,0:T(8,128)(2,1)}) %all-gather.10.cloned.1.call-update) | async-done | bytes 4718608 | tf_op jit(solution)/shard_map/all_gather | solution.py:469
  201.4 80.1 %all-gather.12.cloned.1.call-done.w_down = bf16[3072,768]{1,0:T(8,128)(2,1)} async-done(((bf16[384,768]{1,0:T(8,128)(2,1)}), bf16[3072,768]{1,0:T(8,128)(2,1)}) %all-gather.12.cloned.1.call-update) | async-done | bytes 4718608 | tf_op jit(solution)/shard_map/all_gather | solution.py:469
  281.5 59.9 %mlp.1 = (bf16[1024,768]{1,0:T(8,128)(2,1)}, f32[1024,768]{1,0:T(8,128)}, bf16[1024,768]{1,0:T(8,128)(2,1)}, bf16[768,768]{1,0:T(8,128)(2,1)}, bf16[768,3072]{1,...) custom-call(bf16[1024,768]{1,0:T(8,128)(2,1)} %bitcast.37, ...), custom_call_target="tpu_custom_call" | custom-call | flops 32614907904 | bytes 41943040 | tf_op jit(solution)/shard_map/mlp/pallas_call | solution.py:508
  341.5 33.2 %attend_back.1 = (bf16[2,512,768]{2,1,0:T(8,128)(2,1)}, bf16[2,1456,768]{2,1,0:T(8,128)(2,1)}, bf16[2,1456,768]{2,1,0:T(8,128)(2,1)}) custom-call(s32[2,1456,1]{2,1,0:T(8,128)} %copy.33.codes, s32[2,8,512]{2,1,0:T(8,128)} %add_add_fusion.queries, bf16[2,512,768]{2,1,0:T(8,128)(2,1)} %get-tuple-element.38.q, bf16[2,1456,768]{2,1,0:T(8,128)(2,1)} %get-tuple-element.39.k, ...), custom_call_target="tpu_custom_call" | custom-call | flops 23655874560 | bytes 25165824 | tf_op jit(solution)/shard_map/attend_back/pallas_call | solution.py:526
  374.6 22.7 %qkv_back.1 = (f32[2,512,768]{2,1,0:T(8,128)}, bf16[2,512,768]{2,1,0:T(8,128)(2,1)}, bf16[2,400,768]{2,1,0:T(8,128)(2,1)}, bf16[768,2304]{1,0:T(8,128)(2,1)}, f32[8,2304]{1,0:T(8,128)}) custom-call(s32[2]{0:T(128)} %pad_add_fusion.2.role, bf16[2,1456,768]{2,1,0:T(8,128)(2,1)} %get-tuple-element.43.a, bf16[2,512,768]{2,1,0:T(8,128)(2,1)} %get-tuple-element.46.dq, ...), custom_call_target="tpu_custom_call" | custom-call | flops 14495514624 | bytes 41943040 | tf_op jit(solution)/shard_map/qkv_back/pallas_call | solution.py:536
  399.5 3.5 collective-permute-start.2
  402.9 2.5 collective-permute-done.2
  405.5 1.0 copy-done.2
  406.9 1.2 copy-done.1
  408.1 1.5 fusion
  409.6 2.4 collective-permute-start.3
  412.1 73.5 %reduce-scatter.5.cloned.1.call-done = bf16[96,2304]{1,0:T(8,128)(2,1)} async-done(((bf16[768,2304]{1,0:T(8,128)(2,1)}), bf16[96,2304]{1,0:T(8,128)(2,1)}) %reduce-scatter.5.cloned.1.call-update) | async-done | bytes 442384 | tf_op jit(solution)/shard_map/reduce_scatter | solution.py:567
  485.6 98.6 %reduce-scatter.11.cloned.1.call-done = bf16[384,768]{1,0:T(8,128)(2,1)} async-done(((bf16[3072,768]{1,0:T(8,128)(2,1)}), bf16[384,768]{1,0:T(8,128)(2,1)}) %reduce-scatter.11.cloned.1.call-update) | async-done | bytes 589840 | tf_op jit(solution)/shard_map/reduce_scatter | solution.py:567
  584.2 98.7 %reduce-scatter.9.cloned.1.call-done = bf16[96,3072]{1,0:T(8,128)(2,1)} async-done(((bf16[768,3072]{1,0:T(8,128)(2,1)}), bf16[96,3072]{1,0:T(8,128)(2,1)}) %reduce-scatter.9.cloned.1.call-update) | async-done | bytes 589840 | tf_op jit(solution)/shard_map/reduce_scatter | solution.py:567
  683.9 0.9 slice_reduce_fusion
  686.0 3.4 fusion.2
  689.4 6.9 norm_back.1
  697.4 40.8 %psum.35 = f32[8,1248]{1,0:T(8,128)S(1)} all-reduce(f32[8,1248]{1,0:T(8,128)S(1)} %concatenate.43), channel_id=1, replica_groups=mesh['seq'=4,'fsdp'=8] {'seq','fsdp'}, use_global_device_ids=true, to_apply=%region_0.1 | all-reduce | flops 9984 | bytes 79872 | tf_op jit(solution)/shard_map/psum | solution.py:572
  740.2 2.2 convert_element_type.96
  742.5 2.2 convert_element_type.97
  744.6 1.0 convert_element_type.94
  (94 shorter events, 21.2 us)
Async XLA Ops:
  7.2 53.5 %copy-start = (bf16[2,512,768]{2,1,0:T(8,128)(2,1)S(1)}, bf16[2,512,768]{2,1,0:T(8,128)(2,1)}, u32[]{:S(2)}) copy-start(bf16[2,512,768]{2,1,0:T(8,128)(2,1)} %x.10) | copy-start | bytes 4718596
  7.2 71.4 %all-gather.6.cloned.1.call-start = ((), (), s32[]{:S(2)}) async-start(), calls=%async_computation.4 | async-start | bytes 3981312 | tf_op jit(solution)/shard_map/all_gather | solution.py:469
  7.9 112.6 %all-gather.8.cloned.1.call-start = ((), (), s32[]{:S(2)}) async-start(), calls=%async_computation.5 | async-start | bytes 1327104 | tf_op jit(solution)/shard_map/all_gather | solution.py:469
  8.7 192.8 %all-gather.10.cloned.1.call-start = ((), (), s32[]{:S(2)}) async-start(), calls=%async_computation.6 | async-start | bytes 5308416 | tf_op jit(solution)/shard_map/all_gather | solution.py:469
  9.4 272.1 %all-gather.12.cloned.1.call-start = ((), (), s32[]{:S(2)}) async-start(), calls=%async_computation.7 | async-start | bytes 5308416 | tf_op jit(solution)/shard_map/all_gather | solution.py:469
  10.0 402.1 %reduce-scatter.7.cloned.1.call-start = ((), (), s32[]{:S(2)}) async-start(), calls=%async_computation.9 | async-start | bytes 1327104 | tf_op jit(solution)/shard_map/reduce_scatter | solution.py:567
  10.0 50.6 %collective-permute-start = (bf16[2,512,768]{2,1,0:T(8,128)(2,1)}, bf16[2,512,768]{2,1,0:T(8,128)(2,1)S(1)}, u32[]{:S(2)}, u32[]{:S(2)}) collective-permute-start(bf16[2,512,768]{2,1,0:T(8,128)(2,1)} %x.10), channel_id=1, source_target_pairs={{16,0},{24,8},{17,1},{25,9},{18,2},{26,10},{19,3},{27,11},{20,4},{... | collective-permute-start | bytes 4718600 | tf_op jit(solution)/shard_map/ppermute | solution.py:427
  60.7 1.2 copy-start.6
  60.7 1.1 copy-start.3
  61.8 11.8 %collective-permute-start.1 = (bf16[2,400,768]{2,1,0:T(8,128)(2,1)S(1)}, bf16[2,400,768]{2,1,0:T(8,128)(2,1)}, u32[]{:S(2)}, u32[]{:S(2)}) collective-permute-start(bf16[2,400,768]{2,1,0:T(8,128)(2,1)S(1)} %pad_maximum_fusion), channel_id=1, source_target_pairs={{0,8},{8,0},{16,24},{24,16},{1,9},{9,1},{17,25},{25,17},{2,10},{10... | collective-permute-start | bytes 3686408 | tf_op jit(solution)/shard_map/ppermute | solution.py:430
  341.4 144.2 %reduce-scatter.5.cloned.1.call-start = ((), (), s32[]{:S(2)}) async-start(), calls=%async_computation.8 | async-start | bytes 3981312 | tf_op jit(solution)/shard_map/reduce_scatter | solution.py:567
  397.4 186.9 %reduce-scatter.11.cloned.1.call-start = ((), (), s32[]{:S(2)}) async-start(), calls=%async_computation.11 | async-start | bytes 5308416 | tf_op jit(solution)/shard_map/reduce_scatter | solution.py:567
  398.1 284.8 %reduce-scatter.9.cloned.1.call-start = ((), (), s32[]{:S(2)}) async-start(), calls=%async_computation.10 | async-start | bytes 5308416 | tf_op jit(solution)/shard_map/reduce_scatter | solution.py:567
  398.2 1.3 copy-start.8
  398.9 341.4 %all-reduce.8.cloned.1.call-start = ((), (), s32[]{:S(2)}) async-start(), calls=%async_computation.12 | async-start | bytes 3538944 | tf_op jit(solution)/shard_map/psum | solution.py:567
  399.5 6.0 collective-permute-start.2
  405.5 1.0 copy-start.2
  406.7 1.4 copy-start.1
  408.1 276.8 %copy-start.7 = (f32[8,768]{1,0:T(8,128)S(1)}, f32[8,768]{1,0:T(8,128)}, u32[]{:S(2)}) copy-start(f32[8,768]{1,0:T(8,128)} %get-tuple-element.56) | copy-start | bytes 73732
  409.6 276.4 %collective-permute-start.3 = (bf16[2,512,768]{2,1,0:T(8,128)(2,1)}, bf16[2,512,768]{2,1,0:T(8,128)(2,1)}, u32[]{:S(2)}, u32[]{:S(2)}) collective-permute-start(bf16[2,512,768]{2,1,0:T(8,128)(2,1)} %fusion), channel_id=1, source_target_pairs={{0,16},{8,24},{1,17},{9,25},{2,18},{10,26},{3,19},{11,27},{4,20},{... | collective-permute-start | bytes 4718600 | tf_op jit(solution)/shard_map/ppermute | solution.py:556
  740.2 4.4 copy-start.4
  740.2 5.4 copy-start.5
Sparse Core Ops, SparseCore 0:
  10.2 68.3 all-gather.5
  80.8 39.7 all-gather.7
  122.8 78.6 all-gather.9
  203.5 78.0 all-gather.11
  341.5 62.3 reduce-scatter.6
  407.4 78.0 reduce-scatter.4
  489.2 94.9 reduce-scatter.10
  587.9 95.0 reduce-scatter.8
  685.5 46.9 all-reduce.7

commit v2 on v1

--- a/solution.py
+++ b/solution.py
@@ -1,7 +1,9 @@
 import functools
+import math
 
 import jax
 import jax.numpy as jnp
+import numpy as np
 from jax import lax
 from jax.experimental import pallas as pl
 from jax.experimental.pallas import tpu as pltpu
@@ -17,7 +19,10 @@
 SEG_STEP = 4096
 F32 = jnp.float32
 BF16 = jnp.bfloat16
-VMEM_BYTES = 60 * 1024 * 1024
+VMEM_BYTES = 62 * 1024 * 1024
+MESH = pl.DeviceIdType.MESH
+ANY = pl.BlockSpec(memory_space=pl.ANY)
+VMEM = pl.BlockSpec(memory_space=pltpu.VMEM)
 
 
 def dot(a, b):
@@ -97,23 +102,23 @@
     return noisy, second, pl.multiple_of(own_at, HALO), pl.multiple_of(halo_at, HALO)
 
 
-def qkv_kernel(lay, role, x, xb, xc, w, b, gain, shift, cos, sin, q_out, k_out, v_out, a_out):
+def qkv_rows(lay, where_am, n, x, xb, xc, w, b, gain, shift, cos, sin, q_out, k_out, v_out, a_out):
     width = x.shape[2]
     rows, win = lay["rows"], lay["win"]
-    noisy, second, own_at, halo_at = places(lay, role)
+    noisy, second, own_at, halo_at = where_am
 
     def norm(v):
         normed, _ = norm_stats(v.astype(F32))
-        return (normed * gain[...] + shift[...]).astype(BF16)
+        return (normed * gain + shift).astype(BF16)
 
     def zeros(at, count):
-        k_out[0, at : at + count, :] = jnp.zeros((count, width), BF16)
-        v_out[0, at : at + count, :] = jnp.zeros((count, width), BF16)
+        k_out[n, at : at + count, :] = jnp.zeros((count, width), BF16)
+        v_out[n, at : at + count, :] = jnp.zeros((count, width), BF16)
 
     def section(a, parts, table, want_q):
         def put(ref, col, value):
             for begin, count, at in parts:
-                ref[0, pl.ds(at, count), col : col + value.shape[1]] = value[begin : begin + count]
+                ref[n, pl.ds(at, count), col : col + value.shape[1]] = value[begin : begin + count]
 
         put(a_out, 0, a)
         c = cos[table : table + a.shape[0], :]
@@ -127,7 +132,7 @@
                 if at_col < 2 * width:
                     u = u * c + partner(u) * s
                 if at_col < width:
-                    q_out[0, :, at_col : at_col + 128] = (u[:rows] * (HD**-0.5)).astype(BF16)
+                    q_out[n, :, at_col : at_col + 128] = (u[:rows] * (HD**-0.5)).astype(BF16)
                 elif at_col < 2 * width:
                     put(k_out, at_col - width, u.astype(BF16))
                 else:
@@ -135,12 +140,12 @@
 
     zeros(win + rows, 2 * HALO)
     zeros(lay["keys"] - HALO, HALO)
-    own = jnp.concatenate([norm(x[0]), norm(xc[0, win:, :])], axis=0)
+    own = jnp.concatenate([norm(x[n]), norm(xc[n, win:, :])], axis=0)
     section(own, ((0, rows, own_at), (rows, HALO, halo_at)), win, True)
 
     @pl.when(noisy)
     def _():
-        section(norm(xb[0]), ((0, rows, win),), win, False)
+        section(norm(xb[n]), ((0, rows, win),), win, False)
 
     @pl.when(jnp.logical_not(noisy))
     def _():
@@ -148,11 +153,17 @@
 
     @pl.when(second)
     def _():
-        section(norm(xc[0, :win, :]), ((0, win, 0),), 0, False)
+        section(norm(xc[n, :win, :]), ((0, win, 0),), 0, False)
 
     @pl.when(jnp.logical_not(second))
     def _():
         zeros(0, win)
+
+
+def qkv_kernel(lay, role, x, xb, xc, w, vec, cos, sin, *outs):
+    width = x.shape[2]
+    gain, shift, b = vec[0:1, :width], vec[1:2, :width], vec[2:3, : 3 * width]
+    qkv_rows(lay, places(lay, role), 0, x, xb, xc, w, b, gain, shift, cos, sin, *outs)
 
 
 def windows(lay):
@@ -173,15 +184,15 @@
     return found
 
 
-def make_bias(lay, codes, queries, biases):
+def make_bias(lay, n, codes, queries, biases):
     for t, (lo, hi) in enumerate(windows(lay)):
         here = slice(t * TILE, t * TILE + TILE)
-        low, high, same = (queries[0, n : n + 1, here] for n in range(3))
-        kc = codes[0, lo:hi, :]
+        low, high, same = (queries[n, r : r + 1, here] for r in range(3))
+        kc = codes[n, lo:hi, :]
         ok = (kc >= low) & (kc <= high)
         biases[t][: hi - lo, :] = jnp.where(ok, 0.0, MASKED)
         near = lay["noisy"] + t * TILE
-        kn = codes[0, near : near + NEAR, :]
+        kn = codes[n, near : near + NEAR, :]
         biases[t][hi - lo :, :] = jnp.where(kn == same, 0.0, MASKED)
 
 
@@ -199,27 +210,32 @@
     )
 
 
-def keys_of(ref, lay, t, lo, hi):
+def keys_of(ref, lay, n, cols, t, lo, hi):
     near = lay["noisy"] + t * TILE
-    return jnp.concatenate([ref[0, lo:hi, :], ref[0, near : near + NEAR, :]], axis=0)
-
-
-def attend_kernel(lay, codes, queries, q, k, v, o_out, lse_out, *biases):
-    @pl.when(pl.program_id(1) == 0)
-    def _():
-        make_bias(lay, codes, queries, biases)
-
+    return jnp.concatenate([ref[n, lo:hi, cols], ref[n, near : near + NEAR, cols]], axis=0)
+
+
+def attend(lay, n, cols, q, k, v, o_out, lse_out, lse_at, biases):
     for t, (lo, hi) in enumerate(windows(lay)):
-        qm = stacked(q[0, t * TILE : t * TILE + TILE, :])
-        kk = keys_of(k, lay, t, lo, hi)
-        vv = keys_of(v, lay, t, lo, hi)
+        here = slice(t * TILE, t * TILE + TILE)
+        qm = stacked(q[n, here, cols])
+        kk = keys_of(k, lay, n, cols, t, lo, hi)
+        vv = keys_of(v, lay, n, cols, t, lo, hi)
         s = dot_nt(kk, qm) + jnp.concatenate([biases[t][...]] * QUAD, axis=1)
         peak = jnp.max(s, axis=0, keepdims=True)
         p = jnp.exp(s - peak)
         total = jnp.sum(p, axis=0, keepdims=True)
         wide = dot_tn(vv, p.astype(BF16)) * (1.0 / total)
-        o_out[0, t * TILE : t * TILE + TILE, :] = jnp.transpose(own_heads(wide)).astype(BF16)
-        lse_out[0, 0, t : t + 1, :] = peak + jnp.log(total)
+        o_out[n, here, cols] = jnp.transpose(own_heads(wide)).astype(BF16)
+        lse_out[lse_at, t : t + 1, :] = peak + jnp.log(total)
+
+
+def attend_kernel(lay, codes, queries, q, k, v, o_out, lse_out, *biases):
+    @pl.when(pl.program_id(1) == 0)
+    def _():
+        make_bias(lay, 0, codes, queries, biases)
+
+    attend(lay, 0, slice(None), q, k, v, o_out, lse_out, 0, biases)
 
 
 def attend_back_kernel(
@@ -229,7 +245,7 @@
 
     @pl.when(pl.program_id(1) == 0)
     def _():
-        make_bias(lay, codes, queries, biases)
+        make_bias(lay, 0, codes, queries, biases)
 
     dk_acc[...] = jnp.zeros_like(dk_acc)
     dv_acc[...] = jnp.zeros_like(dv_acc)
@@ -239,15 +255,15 @@
         near = slice(lay["noisy"] + t * TILE, lay["noisy"] + t * TILE + NEAR)
         qm = stacked(q[0, here, :])
         dom = stacked(do[0, here, :])
-        kk = keys_of(k, lay, t, lo, hi)
-        vv = keys_of(v, lay, t, lo, hi)
+        kk = keys_of(k, lay, 0, slice(None), t, lo, hi)
+        vv = keys_of(v, lay, 0, slice(None), t, lo, hi)
         both = jnp.transpose(do[0, here, :].astype(F32) * o[0, here, :].astype(F32))
         delta = jnp.concatenate(
             [jnp.sum(both[h * HD : h * HD + HD, :], axis=0, keepdims=True) for h in range(QUAD)],
             axis=1,
         )
         s = dot_nt(kk, qm) + jnp.concatenate([biases[t][...]] * QUAD, axis=1)
-        p = jnp.exp(s - lse[0, 0, t : t + 1, :])
+        p = jnp.exp(s - lse[0, t : t + 1, :])
         dp = dot_nt(vv, dom)
         ds = (p * (dp - delta)).astype(BF16)
         pb = p.astype(BF16)
@@ -282,27 +298,341 @@
             dk_out[0, here, cols] = (u * c - partner(u) * sn).astype(BF16)
 
 
+def bit_of(index, b):
+    return (index // (1 << b)) % 2
+
+
+def other(index, b):
+    return index + (1 << b) * (1 - 2 * bit_of(index, b))
+
+
+class Net:
+    def __init__(self, bits, send, recv, sems):
+        self.me, self.f, self.bits = lax.axis_index("seq"), lax.axis_index("fsdp"), bits
+        self.core, self.x = self.me % 2, self.me // 2
+        self.send, self.recv, self.sems = send, recv, sems
+        self.used, self.local_used = 0, 0
+        self.started = []
+
+    def partners(self):
+        return [{"seq": other(self.me, 0)}, {"seq": other(self.me, 1)}] + [
+            {"fsdp": other(self.f, b)} for b in range(self.bits)
+        ]
+
+    def barrier(self):
+        barrier = pltpu.get_barrier_semaphore()
+        for device in self.partners():
+            pl.semaphore_signal(barrier, inc=1, device_id=device, device_id_type=MESH)
+        pl.semaphore_wait(barrier, 2 + self.bits)
+
+    def copy(self, src, dst, device):
+        n = self.used
+        self.used += 1
+        return pltpu.make_async_remote_copy(
+            src_ref=src, dst_ref=dst, send_sem=self.send.at[n], recv_sem=self.recv.at[n],
+            device_id=device, device_id_type=MESH,
+        )
+
+    def local(self, src, dst):
+        n = self.local_used
+        self.local_used += 1
+        return pltpu.make_async_copy(src, dst, self.sems.at[n])
+
+    def fsdp_index(self, b):
+        return (slice(None),) * (self.bits - 1 - b) + tuple(
+            bit_of(self.f, low) for low in range(b, -1, -1)
+        )
+
+
+class Gather:
+    def __init__(self, net, own, full, tail, tail_x=None, tail_core=None):
+        self.net, self.at = net, 0
+        mine = net.fsdp_index(net.bits - 1)
+        self.own = net.local(own.at[tail], full.at[mine + tail])
+        self.stages = []
+        for b in range(net.bits - 1, -1, -1):
+            here = full.at[net.fsdp_index(b) + tail]
+            src = own.at[tail] if b == net.bits - 1 else here
+            self.stages.append(net.copy(src, here, {"fsdp": other(net.f, b)}))
+        everything = (slice(None),) * net.bits
+        for region, b in ((tail_x, 1), (tail_core, 0)):
+            if region is not None:
+                here = full.at[everything + region]
+                self.stages.append(net.copy(here, here, {"seq": other(net.me, b)}))
+
+    def advance(self):
+        if self.at == 0:
+            self.own.start()
+        else:
+            self.stages[self.at - 1].wait_recv()
+        if self.at == 1:
+            self.own.wait()
+        if self.at < len(self.stages):
+            self.stages[self.at].start()
+        self.at += 1
+
+    def finish(self):
+        for stage in self.stages:
+            stage.wait_send()
+
+
+def front_kernel(
+    lay, bits, sizes, x, seg, blk, pack, freqs, w_in_s, w_out_s, w_up_s, w_down_s,
+    w_in, w_out, w_up, w_down, q_out, k_out, v_out, a_out, o_out, lse_out, vec, cos, sin, codes, queries,
+    xb, xc, w_vm, q, k, v, a, o, lse, packs, send, recv, sems, *biases,
+):
+    rows, win, length = lay["rows"], lay["win"], lay["length"]
+    width = x.shape[2]
+    hidden = w_up_s.shape[1]
+    micro = x.shape[0]
+    net = Net(bits, send, recv, sems)
+    role = (net.x, net.core)
+    where_am = noisy, second, _, _ = places(lay, role)
+    first = jnp.logical_not(second)
+    clean = jnp.logical_not(noisy)
+    net.barrier()
+
+    pair, across = {"seq": other(net.me, 0)}, {"seq": other(net.me, 1)}
+    rows_across = [net.copy(x.at[n], xb.at[n], across) for n in range(micro)]
+    window = (pl.ds(rows - win, win), slice(None))
+    target = (pl.ds(0, win), slice(None))
+    rows_pair, rows_pair_b = [], []
+    for n in range(micro):
+        at = net.used
+        rows_pair.append(net.copy(x.at[(n,) + window], xc.at[(n,) + target], pair))
+        net.used = at
+        rows_pair_b.append(net.copy(xb.at[(n,) + window], xc.at[(n,) + target], pair))
+    edge_at = pl.multiple_of((1 - net.core) * (rows - HALO), HALO)
+    edge = net.copy(x.at[:, pl.ds(edge_at, HALO), :], xc.at[:, pl.ds(win, HALO), :], pair)
+
+    def columns(begin, size):
+        return (slice(None), pl.ds(pl.multiple_of(begin, 128), size))
+
+    small = Gather(net, pack, packs, (slice(None), slice(None)))
+    half_in, half_out, half_up = 3 * width // 2, width // 2, hidden // 2
+    third = half_in // 3
+    ins = [
+        Gather(net, w_in_s, w_in, columns(net.core * half_in + n * third, third), None,
+               columns(net.core * half_in + n * third, third))
+        for n in range(3)
+    ]
+    out = Gather(net, w_out_s, w_out, columns(net.core * half_out, half_out), None,
+                 columns(net.core * half_out, half_out))
+    quarter = half_up // 2
+    up = Gather(net, w_up_s, w_up, columns(net.core * half_up + net.x * quarter, quarter),
+                columns(net.core * half_up + net.x * quarter, quarter),
+                columns(net.core * half_up, half_up))
+    slab = w_down_s.shape[0]
+    downs = []
+    for n in range(2):
+        region = (pl.ds(pl.multiple_of(net.core * (slab // 2) + n * (slab // 4), HALO), slab // 4), slice(None))
+        downs.append(Gather(net, w_down_s, w_down, region, None, region))
+    down0, down1 = downs
+
+    ins[0].advance()
+    small.advance()
+
+    @pl.when(clean)
+    def _():
+        rows_across[0].start()
+
+    edge.start()
+    ins[1].advance()
+    ins[2].advance()
+
+    position = lax.broadcasted_iota(jnp.int32, (win + rows + HALO, 128), 0)
+    shifted = jnp.where(
+        position < win + rows, position - win, position - win - rows + jnp.where(second, -HALO, rows)
+    )
+    turned = (shifted + jnp.where(second, rows, 0)).astype(F32) * freqs[...]
+    lane = lax.broadcasted_iota(jnp.int32, (win + rows + HALO, 128), 1)
+    cos[...] = jnp.cos(turned)
+    sine = jnp.sin(turned)
+    sin[...] = jnp.where(lane % HD < HD // 2, -sine, sine)
+    code = (seg[...] * SEG_STEP + blk[...]).astype(F32)
+    base = (seg[...] * SEG_STEP).astype(F32)
+    turned_code = jnp.transpose(jnp.concatenate([code, jnp.zeros((8 - micro, length), F32)], axis=0))
+    lay_noisy = lay["noisy"]
+    for n in range(micro):
+        col = turned_code[:, n : n + 1]
+        none = lambda count, value: jnp.full((count, 1), value, F32)
+        codes[n, :win, :] = jnp.where(second, col[rows - win : rows], -1.0)
+        codes[n, win : win + rows, :] = jnp.where(second, col[rows:], col[:rows])
+        after, before = col[rows : rows + HALO], col[rows - HALO : rows]
+        codes[n, win + rows : lay_noisy, :] = jnp.where(jnp.logical_and(clean, first), after, -1.0)
+        codes[n, lay_noisy : lay_noisy + HALO, :] = jnp.where(jnp.logical_and(noisy, second), before, -2.0)
+        codes[n, lay_noisy + HALO : lay_noisy + HALO + rows, :] = jnp.where(
+            noisy, jnp.where(second, col[rows:], col[:rows]), -2.0
+        )
+        codes[n, lay["keys"] - HALO :, :] = jnp.where(jnp.logical_and(noisy, first), after, -2.0)
+        own_code = jnp.where(second, code[n : n + 1, rows:], code[n : n + 1, :rows])
+        own_base = jnp.where(second, base[n : n + 1, rows:], base[n : n + 1, :rows])
+        high = own_code - jnp.where(noisy, 1.0, 0.0)
+        queries[n] = jnp.concatenate([own_base, high, own_code, jnp.zeros((5, rows), F32)], axis=0)
+
+    small.advance()
+    ins[0].advance()
+    ins[1].advance()
+    small.advance()
+    ins[0].advance()
+    ins[2].advance()
+    small.advance()
+
+    count = 1 << bits
+    long_in, long_up = sizes[2] * count, sizes[6] * count
+    spread = {}
+    for size in sorted(set(sizes)):
+        total = jnp.zeros((8, size * count), F32)
+        for n in range(count):
+            at = tuple((n >> b) & 1 for b in range(bits - 1, -1, -1))
+            piece = packs[at]
+            wide = size * count - piece.shape[1]
+            if wide > 0:
+                piece = jnp.concatenate([piece, jnp.zeros((8, wide), F32)], axis=1)
+            lanes = lax.broadcasted_iota(jnp.int32, piece.shape, 1)
+            piece = jnp.where(lanes < size, piece, 0.0)
+            total += pltpu.roll(piece, n * size, 1) if n else piece
+        spread[size] = total
+    for r, size in enumerate(sizes):
+        vec[r : r + 1, : size * count] = spread[size][r : r + 1]
+        if size * count < vec.shape[1]:
+            vec[r : r + 1, size * count :] = jnp.zeros((1, vec.shape[1] - size * count), F32)
+
+    ins[1].advance()
+    up.advance()
+    ins[0].advance()
+    ins[2].advance()
+
+    def pass_on(n):
+        @pl.when(noisy)
+        def _():
+            rows_across[n].wait_recv()
+
+        @pl.when(jnp.logical_and(first, noisy))
+        def _():
+            rows_pair_b[n].start()
+
+        @pl.when(jnp.logical_and(first, clean))
+        def _():
+            rows_pair[n].start()
+
+    @pl.when(clean)
+    def _():
+        rows_across[1].start()
+
+    pass_on(0)
+    ins[1].advance()
+    up.advance()
+    out.advance()
+    ins[2].advance()
+    for n in range(3):
+        ins[n].advance()
+    loads = []
+    for n in range(count):
+        at = tuple((n >> b) & 1 for b in range(bits - 1, -1, -1))
+        loads.append(net.local(w_in.at[at], w_vm.at[pl.ds(n * w_in_s.shape[0], w_in_s.shape[0]), :]))
+    for load in loads:
+        load.start()
+    edge.wait_recv()
+    up.advance()
+    out.advance()
+    down0.advance()
+    for load in loads:
+        load.wait()
+
+    gain, shift, b_in = vec[0:1, :width], vec[1:2, :width], vec[2:3, : 3 * width]
+
+    def qkv(n):
+        @pl.when(second)
+        def _():
+            rows_pair[n].wait_recv()
+
+        qkv_rows(lay, where_am, n, x, xb, xc, w_vm, b_in, gain, shift, cos, sin, q, k, v, a)
+        stores = [
+            net.local(here.at[n], there.at[n])
+            for here, there in ((q, q_out), (k, k_out), (v, v_out), (a, a_out))
+        ]
+        for store in stores:
+            store.start()
+        return stores
+
+    stores = qkv(0)
+    down0.advance()
+    out.advance()
+    pass_on(1)
+    down1.advance()
+    stores += qkv(1)
+
+    quads = width // (QUAD * HD)
+    plan = ((up, down0, out), (down1,), (down0, down1), (up,), (out, down0, down1), (up,))
+    assert micro * quads == len(plan)
+
+    def step(index, carry):
+        n, h = index // quads, index % quads
+
+        @pl.when(h == 0)
+        def _():
+            make_bias(lay, n, codes, queries, biases)
+
+        cols = pl.ds(pl.multiple_of(h * QUAD * HD, QUAD * HD), QUAD * HD)
+        attend(lay, n, cols, q, k, v, o, lse, index, biases)
+        for at, chunks in enumerate(plan):
+
+            @pl.when(index == at)
+            def _():
+                for chunk in chunks:
+                    chunk.advance()
+
+        return carry
+
+    lax.fori_loop(0, micro * quads, step, 0)
+    last = [net.local(o, o_out), net.local(lse, lse_out)]
+    for store in last:
+        store.start()
+    chunks = [small, out, up, down0, down1] + ins
+    for chunk in chunks:
+        while chunk.at <= len(chunk.stages):
+            chunk.advance()
+    for chunk in chunks:
+        chunk.finish()
+    for store in stores + last:
+        store.wait()
+    edge.wait_send()
+
+    @pl.when(clean)
+    def _():
+        for n in range(micro):
+            rows_across[n].wait_send()
+
+    @pl.when(first)
+    def _():
+        for n in range(micro):
+            rows_pair[n].wait_send()
+
+
 def mlp_kernel(
-    o, x, dy, w_out, b_out, gain, shift, w_up, b_up, w_down, b_down,
+    o, x, dy, w_out, vec, w_up, b_up, w_down,
     out_rows, dx2_out, do_out, g_w_out, g_w_up, g_b_up, g_w_down, g_vec,
     mid, a2, a2t, inv, acc_out, acc_da,
 ):
     step = pl.program_id(0)
     last = pl.num_programs(0) - 1
+    width = x.shape[1]
+    b_out, gain, shift, b_down = (vec[r : r + 1, :width] for r in (3, 4, 5, 7))
 
     @pl.when(step == 0)
     def _():
-        value = x[...].astype(F32) + dot(o[...], w_out[...]) + b_out[...]
+        value = x[...].astype(F32) + dot(o[...], w_out[...]) + b_out
         mid[...] = value
         normed, inverse = norm_stats(value)
         inv[...] = inverse
-        a = (normed * gain[...] + shift[...]).astype(BF16)
+        a = (normed * gain + shift).astype(BF16)
         a2[...] = a
         a2t[...] = jnp.transpose(a)
         acc_out[...] = jnp.zeros_like(acc_out)
         acc_da[...] = jnp.zeros_like(acc_da)
 
-    u = dot(a2[...], w_up[...]) + b_up[...]
+    u = dot(a2[...], w_up[...]) + b_up[6:7, :]
     scale = 0.7978845608028654
     square = u * u
     inner = scale * u * (1.0 + 0.044715 * square)
@@ -321,12 +651,12 @@
     @pl.when(step == last)
     def _():
         dyf = dy[...].astype(F32)
-        out_rows[...] = (mid[...] + acc_out[...] + b_down[...]).astype(BF16)
+        out_rows[...] = (mid[...] + acc_out[...] + b_down).astype(BF16)
         inverse = inv[...]
         value = mid[...]
         normed = (value - jnp.mean(value, axis=-1, keepdims=True)) * inverse
         da = acc_da[...]
-        dx2 = dyf + norm_back(da, normed, inverse, gain[...])
+        dx2 = dyf + norm_back(da, normed, inverse, gain)
         dx2_out[...] = dx2
         dp = dx2.astype(BF16)
         do_out[...] = dot_nt(dp, w_out[...]).astype(BF16)
@@ -404,6 +734,117 @@
 
     g_vec[0:1, :] += jnp.sum(grad * normed, axis=0, keepdims=True)
     g_vec[1:2, :] += jnp.sum(grad, axis=0, keepdims=True)
+
+
+def front_remote(
+    lay, role, sizes, inputs, segment_ids, block_ids, small, weights, freqs, lse_shape, bias_scratch, spans, attn_flops
+):
+    micro, rows, width = inputs.shape
+    keys, win = lay["keys"], lay["win"]
+    bits = lax.axis_size("fsdp").bit_length() - 1
+    lanes = -(-max(sizes) // 128) * 128
+    pack = jnp.stack([jnp.pad(p.astype(F32), (0, lanes - p.shape[0])) for p in small])
+    full = [like((2,) * bits + p.shape, BF16) for p in weights]
+    longest = max(sizes) << bits
+    table_rows = win + rows + HALO
+    shapes = full + [
+        like((micro, rows, width), BF16), like((micro, keys, width), BF16), like((micro, keys, width), BF16),
+        like((micro, keys, width), BF16), like((micro, rows, width), BF16), like(lse_shape, F32),
+        like((8, longest), F32), like((table_rows, 128), F32), like((table_rows, 128), F32),
+        like((micro, keys, 1), F32), like((micro, 8, rows), F32),
+    ]
+    remote = 3 * micro + 1 + bits * 8 + 10
+    outs = pl.pallas_call(
+        functools.partial(front_kernel, lay, bits, sizes),
+        in_specs=[VMEM] * 9,
+        out_specs=[ANY] * 10 + [VMEM] * 5,
+        out_shape=shapes,
+        scratch_shapes=[
+            pltpu.VMEM((micro, rows, width), BF16), pltpu.VMEM((micro, win + HALO, width), BF16),
+            pltpu.VMEM((width, 3 * width), BF16), pltpu.VMEM((micro, rows, width), BF16),
+            pltpu.VMEM((micro, keys, width), BF16), pltpu.VMEM((micro, keys, width), BF16),
+            pltpu.VMEM((micro, keys, width), BF16), pltpu.VMEM((micro, rows, width), BF16),
+            pltpu.VMEM(lse_shape, F32), pltpu.VMEM((2,) * bits + (8, lanes), F32),
+            pltpu.SemaphoreType.DMA((remote,)), pltpu.SemaphoreType.DMA((remote,)),
+            pltpu.SemaphoreType.DMA((32,)),
+        ] + bias_scratch,
+        compiler_params=pltpu.CompilerParams(
+            vmem_limit_bytes=VMEM_BYTES, collective_id=0, has_side_effects=True
+        ),
+        cost_estimate=pl.CostEstimate(flops=2 * attn_flops, bytes_accessed=40 << 20, transcendentals=0),
+        name="front",
+    )(inputs, segment_ids, block_ids, pack, freqs, *weights)
+    joined = [w.reshape((-1, w.shape[-1])) for w in outs[:4]]
+    return tuple(joined) + tuple(outs[4:])
+
+
+def front_native(
+    lay, role, sizes, inputs, segment_ids, block_ids, small, weights, freqs, lse_shape, bias_scratch, spans, attn_flops
+):
+    micro, rows, width = inputs.shape
+    keys, win, length = lay["keys"], lay["win"], lay["length"]
+    clean, half = role[0], role[1]
+    pairs = [(0, 1), (1, 0), (2, 3), (3, 2)]
+    xb = lax.ppermute(inputs, "seq", [(2, 0), (3, 1)])
+    xmain = jnp.where(clean == 1, inputs, xb)
+    edge = jnp.where(half == 0, inputs[:, rows - HALO :], inputs[:, :HALO])
+    xc = lax.ppermute(jnp.concatenate([xmain[:, rows - win :], edge], axis=1), "seq", pairs)
+    start = half * rows
+    edge_at = jnp.where(half == 0, rows, -HALO)
+    positions = start + jnp.concatenate([jnp.arange(-win, rows), edge_at + jnp.arange(HALO)])
+    turned = positions.astype(F32)[:, None] * freqs
+    sine = jnp.sin(turned)
+    cos = jnp.cos(turned)
+    sin = jnp.where(jnp.arange(128)[None] % HD < HD // 2, -sine, sine)
+    code = segment_ids * SEG_STEP + block_ids
+    padded = jnp.pad(code, ((0, 0), (win, 0)), constant_values=-1)
+    key_codes = lax.dynamic_slice_in_dim(padded, start, win + rows, 1)
+    own_code = lax.dynamic_slice_in_dim(code, start, rows, 1)
+    own_seg = lax.dynamic_slice_in_dim(segment_ids, start, rows, 1)
+    before, after = code[:, rows - HALO : rows], code[:, rows : rows + HALO]
+    codes = jnp.concatenate(
+        [
+            key_codes,
+            jnp.where((clean == 1) & (half == 0), after, -1),
+            jnp.where((clean == 0) & (half == 1), before, -2),
+            jnp.where(clean == 0, own_code, -2),
+            jnp.where((clean == 0) & (half == 0), after, -2),
+        ],
+        axis=1,
+    )[:, :, None].astype(F32)
+    queries = jnp.stack([own_seg * SEG_STEP, own_code - (1 - clean), own_code], axis=1)
+    queries = jnp.concatenate([queries, jnp.zeros((micro, 5, rows), jnp.int32)], axis=1).astype(F32)
+    packed = lax.all_gather(jnp.concatenate(small)[None], "fsdp", axis=0, tiled=True)
+    vectors, at = [], 0
+    longest = max(sizes) * packed.shape[0]
+    for size in sizes:
+        one = packed[:, at : at + size].reshape(-1).astype(F32)
+        vectors.append(jnp.pad(one, (0, longest - one.shape[0])))
+        at += size
+    vec = jnp.stack(vectors)
+    w_in, w_out, w_up, w_down = (lax.all_gather(p, "fsdp", axis=0, tiled=True) for p in weights)
+    per_seq = lambda n, d: pl.BlockSpec((1, n, d), lambda s: (s, 0, 0))
+    table_rows = win + rows + HALO
+    q, k, v, a = call(
+        functools.partial(qkv_kernel, lay), (micro,),
+        [SMEM(), per_seq(rows, width), per_seq(rows, width), per_seq(win + HALO, width),
+         whole((width, 3 * width)), whole(vec.shape), whole((table_rows, 128)), whole((table_rows, 128))],
+        [per_seq(rows, width), per_seq(keys, width), per_seq(keys, width), per_seq(keys, width)],
+        [like((micro, rows, width), BF16)] + [like((micro, keys, width), BF16)] * 3,
+        [], 2 * micro * rows * width * 3 * width * 2, 20 << 20, "qkv",
+    )(role, inputs, xb, xc, w_in, vec, cos, sin)
+    qw = QUAD * HD
+    quads = width // qw
+    quad_block = lambda n: pl.BlockSpec((1, n, qw), lambda s, h: (s, 0, h))
+    o, lse = call(
+        functools.partial(attend_kernel, lay), (micro, quads),
+        [pl.BlockSpec((1, keys, 1), lambda s, h: (s, 0, 0)), pl.BlockSpec((1, 8, rows), lambda s, h: (s, 0, 0)),
+         quad_block(rows), quad_block(keys), quad_block(keys)],
+        [quad_block(rows), pl.BlockSpec((1,) + lse_shape[1:], lambda s, h: (s * quads + h, 0, 0))],
+        [like((micro, rows, width), BF16), like(lse_shape, F32)],
+        bias_scratch, 2 * attn_flops, 12 << 20, "attend",
+    )(codes, queries, q, k, v)
+    return w_in, w_out, w_up, w_down, q, k, v, a, o, lse, vec, cos, sin, codes, queries
 
 
 def per_device(
@@ -423,93 +864,41 @@
     half = me % 2
     role = jnp.stack([clean, half]).astype(jnp.int32)
     pairs = [(0, 1), (1, 0), (2, 3), (3, 2)]
-
-    xb = lax.ppermute(inputs, "seq", [(2, 0), (3, 1)])
-    xmain = jnp.where(clean == 1, inputs, xb)
-    edge = jnp.where(half == 0, inputs[:, rows - HALO :], inputs[:, :HALO])
-    xc = lax.ppermute(jnp.concatenate([xmain[:, rows - win :], edge], axis=1), "seq", pairs)
-
-    start = half * rows
-    edge_at = jnp.where(half == 0, rows, -HALO)
-    positions = start + jnp.concatenate([jnp.arange(-win, rows), edge_at + jnp.arange(HALO)])
-    freqs = 10000.0 ** (-(jnp.arange(HD // 2, dtype=F32) / (HD // 2)))
-    turned = positions.astype(F32)[:, None] * freqs[None, :]
-    cosine, sine = jnp.cos(turned), jnp.sin(turned)
-    cos = jnp.concatenate([cosine] * 4, axis=1)
-    sin = jnp.concatenate([-sine, sine] * 2, axis=1)
-
-    code = segment_ids * SEG_STEP + block_ids
-    padded = jnp.pad(code, ((0, 0), (win, 0)), constant_values=-1)
-    key_codes = lax.dynamic_slice_in_dim(padded, start, win + rows, 1)
-    own_code = lax.dynamic_slice_in_dim(code, start, rows, 1)
-    own_seg = lax.dynamic_slice_in_dim(segment_ids, start, rows, 1)
-    before, after = code[:, rows - HALO : rows], code[:, rows : rows + HALO]
-    codes = jnp.concatenate(
-        [
-            key_codes,
-            jnp.where((clean == 1) & (half == 0), after, -1),
-            jnp.where((clean == 0) & (half == 1), before, -2),
-            jnp.where(clean == 0, own_code, -2),
-            jnp.where((clean == 0) & (half == 0), after, -2),
-        ],
-        axis=1,
-    )[:, :, None]
-    queries = jnp.stack([own_seg * SEG_STEP, own_code - (1 - clean), own_code], axis=1)
-    queries = jnp.concatenate([queries, jnp.zeros((micro, 5, rows), jnp.int32)], axis=1)
-
     small = (attn_gain, attn_shift, bias_in, bias_out, mlp_gain, mlp_shift, bias_up, bias_down)
     sizes = [p.shape[0] for p in small]
-    packed = lax.all_gather(jnp.concatenate(small)[None], "fsdp", axis=0, tiled=True)
-    vectors, at = [], 0
-    for size in sizes:
-        vectors.append(packed[:, at : at + size].reshape(1, -1).astype(F32))
-        at += size
-    gain1, shift1, b_in, b_out, gain2, shift2, b_up, b_down = vectors
-    w_in, w_out, w_up, w_down = (
-        lax.all_gather(p, "fsdp", axis=0, tiled=True)
-        for p in (proj_in, proj_out, weight_up, weight_down)
-    )
-
+    weights = (proj_in, proj_out, weight_up, weight_down)
+    half_dim = HD // 2
+    freqs = (10000.0 ** (-(np.arange(half_dim, dtype=np.float32) / half_dim))).astype(np.float32)
+    freqs = np.tile(freqs, 4)[None]
     quads = width // (QUAD * HD)
     qw = QUAD * HD
     spans = [hi - lo + NEAR for lo, hi in windows(lay)]
     bias_scratch = [pltpu.VMEM((n, TILE), F32) for n in spans]
     per_seq = lambda n, d: pl.BlockSpec((1, n, d), lambda s: (s, 0, 0))
     role_spec = SMEM()
-
-    q, k, v, a = call(
-        functools.partial(qkv_kernel, lay), (micro,),
-        [role_spec, per_seq(rows, width), per_seq(rows, width), per_seq(win + HALO, width),
-         whole((width, 3 * width)), whole((1, 3 * width)), whole((1, width)), whole((1, width)),
-         whole((win + rows + HALO, 128)), whole((win + rows + HALO, 128))],
-        [per_seq(rows, width), per_seq(keys, width), per_seq(keys, width), per_seq(keys, width)],
-        [like((micro, rows, width), BF16)] + [like((micro, keys, width), BF16)] * 3,
-        [], 2 * micro * rows * width * 3 * width * 2, 20 << 20, "qkv",
-    )(role, inputs, xb, xc, w_in, b_in, gain1, shift1, cos, sin)
-
+    attn_flops = micro * quads * sum(spans) * QUAD * TILE * qw * 2
+    lse_shape = (micro * quads, rows // TILE, QUAD * TILE)
+    table_rows = win + rows + HALO
+    aligned = fsdp_n & (fsdp_n - 1) == 0 and all(p.shape[0] % (4 * HALO) in (0, 32) for p in weights)
+    front = front_remote if aligned else front_native
+    (w_in, w_out, w_up, w_down, q, k, v, a, o, lse, vec, cos, sin, codes, queries) = front(
+        lay, role, sizes, inputs, segment_ids, block_ids, small, weights, freqs,
+        lse_shape, bias_scratch, spans, attn_flops,
+    )
     quad_block = lambda n: pl.BlockSpec((1, n, qw), lambda s, h: (s, 0, h))
     code_spec = pl.BlockSpec((1, keys, 1), lambda s, h: (s, 0, 0))
     query_spec = pl.BlockSpec((1, 8, rows), lambda s, h: (s, 0, 0))
-    lse_spec = pl.BlockSpec((1, 1, rows // TILE, QUAD * TILE), lambda s, h: (s, h, 0, 0))
-    attn_flops = micro * quads * sum(spans) * QUAD * TILE * qw * 2
-    o, lse = call(
-        functools.partial(attend_kernel, lay), (micro, quads),
-        [code_spec, query_spec, quad_block(rows), quad_block(keys), quad_block(keys)],
-        [quad_block(rows), lse_spec],
-        [like((micro, rows, width), BF16), like((micro, quads, rows // TILE, QUAD * TILE), F32)],
-        bias_scratch, 2 * attn_flops, 12 << 20, "attend",
-    )(codes, queries, q, k, v)
+    lse_spec = pl.BlockSpec((1,) + lse_shape[1:], lambda s, h: (s * quads + h, 0, 0))
 
     total = micro * rows
     flat = lambda z: z.reshape(total, width)
     chunk = min(512, hidden)
-    vec = whole((1, width))
     rows_spec = whole((total, width))
     out_rows, dx2, do, g_w_out, g_w_up, g_b_up, g_w_down, g_mlp = call(
         mlp_kernel, (hidden // chunk,),
-        [rows_spec, rows_spec, rows_spec, whole((width, width)), vec, vec, vec,
-         pl.BlockSpec((width, chunk), lambda j: (0, j)), pl.BlockSpec((1, chunk), lambda j: (0, j)),
-         pl.BlockSpec((chunk, width), lambda j: (j, 0)), vec],
+        [rows_spec, rows_spec, rows_spec, whole((width, width)), whole(vec.shape),
+         pl.BlockSpec((width, chunk), lambda j: (0, j)), pl.BlockSpec((8, chunk), lambda j: (0, j)),
+         pl.BlockSpec((chunk, width), lambda j: (j, 0))],
         [rows_spec, rows_spec, rows_spec, whole((width, width)),
          pl.BlockSpec((width, chunk), lambda j: (0, j)), pl.BlockSpec((8, chunk), lambda j: (0, j)),
          pl.BlockSpec((chunk, width), lambda j: (j, 0)), whole((8, width))],
@@ -519,10 +908,10 @@
         [pltpu.VMEM((total, width), F32), pltpu.VMEM((total, width), BF16), pltpu.VMEM((width, total), BF16),
          pltpu.VMEM((total, 1), F32), pltpu.VMEM((total, width), F32), pltpu.VMEM((total, width), F32)],
         2 * total * width * (6 * hidden + 3 * width), 40 << 20, "mlp",
-    )(flat(o), flat(inputs), flat(cotangent), w_out, b_out, gain2, shift2, w_up, b_up, w_down, b_down)
+    )(flat(o), flat(inputs), flat(cotangent), w_out, vec, w_up, vec, w_down)
 
     seqs = lambda z: z.reshape(micro, rows, width)
-    table = pl.BlockSpec((win + rows + HALO, 128), lambda s, h: (0, 0), pipeline_mode=pl.Buffered(1))
+    table = pl.BlockSpec((table_rows, 128), lambda s, h: (0, 0), pipeline_mode=pl.Buffered(1))
     dq, dk, dv = call(
         functools.partial(attend_back_kernel, lay), (micro, quads),
         [code_spec, query_spec, quad_block(rows), quad_block(keys), quad_block(keys),
@@ -558,10 +947,10 @@
 
     grad_in, g_attn = call(
         final_kernel, (2,),
-        [pl.BlockSpec((total // 2, width), lambda i: (i, 0))] * 4 + [vec],
+        [pl.BlockSpec((total // 2, width), lambda i: (i, 0))] * 4 + [whole((1, width))],
         [pl.BlockSpec((total // 2, width), lambda i: (i, 0)), whole((8, width))],
         [like((total, width), F32), like((8, width), F32)], [], 0, 16 << 20, "norm_back",
-    )(flat(inputs), flat(da_own), flat(extra), dx2, gain1)
+    )(flat(inputs), flat(da_own), flat(extra), dx2, vec[0:1, :width])
 
     def scatter(g):
         return lax.psum(lax.psum_scatter(g, "fsdp", scatter_dimension=0, tiled=True), "seq")

time: 756 us -> 582 us (0.77)
  waiting for transfers between devices: 446 us -> 271 us
  Pallas kernels: 162 us -> 209 us
  blocking collectives: 80.5 us -> 40.8 us
  local copies, waits for them, and re-layouts: 24 us -> 15.8 us
    all_gather x4 -> x0, waiting for transfers between devices: 168 us -> none  [per_device(): lax.all_gather(p, 'fsdp', axis=0, tiled=True)]
    pallas_call x2 -> x1, Pallas kernels: 39.6 us -> 97.5 us  [front_remote(): pl.pallas_call(functools.partial(front_kernel, lay, bits, sizes), in_spec...]
    unnamed x1 -> x0, blocking collectives: 39.7 us -> none
    pallas_call x1, Pallas kernels: 59.9 us -> 48.7 us  [per_device(): call(mlp_kernel, (hidden // chunk,), [rows_spec, rows_spec, rows_spec, wh...]
  transfers between devices with their start and end apart: 13 -> 7, of which waited for: 8 -> 4; matrix products, arithmetic and copies ran while one was open for 4% -> 2% of each run, Pallas kernels for 14% -> 11%
where the time goes in v2:
time: 582 us; the launch traced here: 573 us
  waiting for transfers between devices  271 us (47%)
  Pallas kernels  209 us (36%)
  blocking collectives  40.8 us (7%)
  local copies, waits for them, and re-layouts  15.8 us (3%)
  between operations  14.1 us (2%)
  other arithmetic  12.6 us (2%)
  starting transfers between devices  9.36 us (2%)
    reduce_scatter x4, waiting for transfers between devices, scatter(): lax.psum_scatter(g, 'fsdp', scatter_dimension=0, tiled=True)  268 us
    pallas_call x1, Pallas kernels, front_remote(): pl.pallas_call(functools.partial(front_kernel, lay, bits, sizes), in_spec...  97.5 us
    pallas_call x1, Pallas kernels, per_device(): call(mlp_kernel, (hidden // chunk,), [rows_spec, rows_spec, rows_spec, wh...  48.7 us
    psum x1, blocking collectives, per_device(): pack = lax.psum(pack, ('seq', 'fsdp'))  40.8 us
    pallas_call x1, Pallas kernels, per_device(): call(functools.partial(attend_back_kernel, lay), (micro, quads), [code_sp...  33.3 us
    pallas_call x1, Pallas kernels, per_device(): call(functools.partial(qkv_back_kernel, lay), (micro,), [role_spec, per_s...  22.7 us
  transfers between devices with their start and end apart: 7, of which 4 were waited for; matrix products, arithmetic and copies ran while one was open for 2% of the time, Pallas kernels for 11%

profile of v2, /device:TPU:0, one launch (start us, length us, event | category | flops | bytes accessed | tf_op | source)
XLA Modules:
  0.0 573.1 jit_solution(3656685417210733934)
XLA Ops:
  7.2 0.7 pad.36
  8.6 0.7 pad.38
  11.9 0.7 stack.52
  13.2 97.5 %front.1 = (bf16[2,2,2,96,2304]{4,3,2,1,0:T(8,128)(2,1)}, bf16[2,2,2,96,768]{4,3,2,1,0:T(8,128)(2,1)}, bf16[2,2,2,96,3072]{4,3,2,1,0:T(8,128)(2,1)}, bf16[2,2,2,...) custom-call(bf16[2,512,768]{2,1,0:T(8,128)(2,1)} %x.21, ...), custom_call_target="tpu_custom_call" | custom-call | flops 9462349824 | bytes 41943040 | tf_op jit(solution)/shard_map/front/pallas_call | solution.py:757
  110.8 48.7 %mlp.1 = (bf16[1024,768]{1,0:T(8,128)(2,1)}, f32[1024,768]{1,0:T(8,128)}, bf16[1024,768]{1,0:T(8,128)(2,1)}, bf16[768,768]{1,0:T(8,128)(2,1)}, bf16[768,3072]{1,...) custom-call(bf16[1024,768]{1,0:T(8,128)(2,1)} %bitcast.36, ...), custom_call_target="tpu_custom_call" | custom-call | flops 32614907904 | bytes 41943040 | tf_op jit(solution)/shard_map/mlp/pallas_call | solution.py:897
  159.6 33.3 %attend_back.1 = (bf16[2,512,768]{2,1,0:T(8,128)(2,1)}, bf16[2,1456,768]{2,1,0:T(8,128)(2,1)}, bf16[2,1456,768]{2,1,0:T(8,128)(2,1)}) custom-call(f32[2,1456,1]{2,1,0:T(8,128)} %get-tuple-element.54.codes, f32[2,8,512]{2,1,0:T(8,128)} %get-tuple-element.55.queries, bf16[2,512,768]{2,1,0:T(8,128)(2,1)} %get-tuple-element.56.q, ...), custom_call_target="tpu_custom_call" | custom-call | flops 23655874560 | bytes 25165824 | tf_op jit(solution)/shard_map/attend_back/pallas_call | solution.py:915
  193.4 22.7 %qkv_back.1 = (f32[2,512,768]{2,1,0:T(8,128)}, bf16[2,512,768]{2,1,0:T(8,128)(2,1)}, bf16[2,400,768]{2,1,0:T(8,128)(2,1)}, bf16[768,2304]{1,0:T(8,128)(2,1)}, f32[8,2304]{1,0:T(8,128)}) custom-call(s32[2]{0:T(128)} %pad_add_fusion.2.role, bf16[2,1456,768]{2,1,0:T(8,128)(2,1)} %get-tuple-element.53.a, bf16[2,512,768]{2,1,0:T(8,128)(2,1)} %get-tuple-element.63.dq, ...), custom_call_target="tpu_custom_call" | custom-call | flops 14495514624 | bytes 41943040 | tf_op jit(solution)/shard_map/qkv_back/pallas_call | solution.py:925
  216.2 0.7 reduce-scatter.11.cloned.1.call-update
  217.5 0.7 copy-done.5
  218.1 6.7 %collective-permute-start = (bf16[2,400,768]{2,1,0:T(8,128)(2,1)S(1)}, bf16[2,400,768]{2,1,0:T(8,128)(2,1)S(1)}, u32[]{:S(2)}, u32[]{:S(2)}) collective-permute-start(bf16[2,400,768]{2,1,0:T(8,128)(2,1)S(1)} %copy-done.5), channel_id=1, source_target_pairs={{0,8},{8,0},{16,24},{24,16},{1,9},{9,1},{17,25},{25,17},{2,10},{10... | collective-permute-start | bytes 3686408 | tf_op jit(solution)/shard_map/ppermute | solution.py:936
  224.9 2.5 collective-permute-done
  227.4 1.1 copy-done.1
  228.8 1.2 copy-done
  230.1 1.5 fusion
  231.6 2.4 collective-permute-start.1
  234.1 1.3 slice.83.gain
  235.4 70.3 %reduce-scatter.5.cloned.1.call-done = bf16[96,2304]{1,0:T(8,128)(2,1)} async-done(((bf16[768,2304]{1,0:T(8,128)(2,1)}), bf16[96,2304]{1,0:T(8,128)(2,1)}) %reduce-scatter.5.cloned.1.call-update) | async-done | bytes 442384 | tf_op jit(solution)/shard_map/reduce_scatter | solution.py:956
  305.7 98.5 %reduce-scatter.11.cloned.1.call-done = bf16[384,768]{1,0:T(8,128)(2,1)} async-done(((bf16[3072,768]{1,0:T(8,128)(2,1)}), bf16[384,768]{1,0:T(8,128)(2,1)}) %reduce-scatter.11.cloned.1.call-update) | async-done | bytes 589840 | tf_op jit(solution)/shard_map/reduce_scatter | solution.py:956
  404.2 98.7 %reduce-scatter.9.cloned.1.call-done = bf16[96,3072]{1,0:T(8,128)(2,1)} async-done(((bf16[768,3072]{1,0:T(8,128)(2,1)}), bf16[96,3072]{1,0:T(8,128)(2,1)}) %reduce-scatter.9.cloned.1.call-update) | async-done | bytes 589840 | tf_op jit(solution)/shard_map/reduce_scatter | solution.py:956
  503.0 0.9 slice_reduce_fusion.1
  504.3 0.9 slice_reduce_fusion
  505.2 0.8 slice.109
  506.1 3.4 fusion.2
  509.5 6.9 %norm_back.1 = (f32[1024,768]{1,0:T(8,128)}, f32[8,768]{1,0:T(8,128)}) custom-call(bf16[1024,768]{1,0:T(8,128)(2,1)} %bitcast.29, f32[1024,768]{1,0:T(8,128)} %bitcast.27, f32[1024,768]{1,0:T(8,128)} %bitcast.26, f32[1024,768]{1,0:T(8,128)} %get-tuple-element.70.dx2, f32[1,768]{1,0:T(1,128)} %slice.83.gain), custom_call_target="tpu_custom_call" | custom-call | bytes 16777216 | tf_op jit(solution)/shard_map/norm_back/pallas_call | solution.py:948
  516.4 0.8 slice_reduce_fusion.6
  517.5 40.8 %psum.35 = f32[8,1248]{1,0:T(8,128)S(1)} all-reduce(f32[8,1248]{1,0:T(8,128)S(1)} %concatenate.11), channel_id=1, replica_groups=mesh['seq'=4,'fsdp'=8] {'seq','fsdp'}, use_global_device_ids=true, to_apply=%region_0.1 | all-reduce | flops 9984 | bytes 79872 | tf_op jit(solution)/shard_map/psum | solution.py:961
  558.4 0.7 dynamic-slice_reduce_fusion
  559.0 0.7 dynamic-slice_reduce_fusion.1
  560.3 2.2 convert_element_type.49
  562.6 2.2 convert_element_type.50
  564.7 1.0 convert_element_type.47
  565.7 0.7 convert_element_type.48
  (49 shorter events, 6.9 us)
Async XLA Ops:
  7.2 228.2 %reduce-scatter.7.cloned.1.call-start = ((), (), s32[]{:S(2)}) async-start(), calls=%async_computation.5 | async-start | bytes 1327104 | tf_op jit(solution)/shard_map/reduce_scatter | solution.py:956
  159.5 146.2 %reduce-scatter.5.cloned.1.call-start = ((), (), s32[]{:S(2)}) async-start(), calls=%async_computation.4 | async-start | bytes 3981312 | tf_op jit(solution)/shard_map/reduce_scatter | solution.py:956
  216.1 188.1 %reduce-scatter.11.cloned.1.call-start = ((), (), s32[]{:S(2)}) async-start(), calls=%async_computation.7 | async-start | bytes 5308416 | tf_op jit(solution)/shard_map/reduce_scatter | solution.py:956
  216.8 1.3 copy-start.5
  216.9 286.1 %reduce-scatter.9.cloned.1.call-start = ((), (), s32[]{:S(2)}) async-start(), calls=%async_computation.6 | async-start | bytes 5308416 | tf_op jit(solution)/shard_map/reduce_scatter | solution.py:956
  217.4 342.9 %all-reduce.13.cloned.1.call-start = ((), (), s32[]{:S(2)}) async-start(), calls=%async_computation.8 | async-start | bytes 3538944 | tf_op jit(solution)/shard_map/psum | solution.py:956
  218.1 9.3 %collective-permute-start = (bf16[2,400,768]{2,1,0:T(8,128)(2,1)S(1)}, bf16[2,400,768]{2,1,0:T(8,128)(2,1)S(1)}, u32[]{:S(2)}, u32[]{:S(2)}) collective-permute-start(bf16[2,400,768]{2,1,0:T(8,128)(2,1)S(1)} %copy-done.5), channel_id=1, source_target_pairs={{0,8},{8,0},{16,24},{24,16},{1,9},{9,1},{17,25},{25,17},{2,10},{10... | collective-permute-start | bytes 3686408 | tf_op jit(solution)/shard_map/ppermute | solution.py:936
  227.4 1.1 copy-start.1
  228.7 1.4 copy-start
  230.1 273.9 %copy-start.4 = (f32[8,768]{1,0:T(8,128)S(1)}, f32[8,768]{1,0:T(8,128)}, u32[]{:S(2)}) copy-start(f32[8,768]{1,0:T(8,128)} %get-tuple-element.74) | copy-start | bytes 73732
  231.6 274.4 %collective-permute-start.1 = (bf16[2,512,768]{2,1,0:T(8,128)(2,1)}, bf16[2,512,768]{2,1,0:T(8,128)(2,1)}, u32[]{:S(2)}, u32[]{:S(2)}) collective-permute-start(bf16[2,512,768]{2,1,0:T(8,128)(2,1)} %fusion), channel_id=1, source_target_pairs={{0,16},{8,24},{1,17},{9,25},{2,18},{10,26},{3,19},{11,27},{4,20},{... | collective-permute-start | bytes 4718600 | tf_op jit(solution)/shard_map/ppermute | solution.py:945
  560.3 4.4 copy-start.2
  560.3 5.4 copy-start.3
Sparse Core Ops, SparseCore 0:
  159.6 64.3 reduce-scatter.6
  227.6 78.0 reduce-scatter.4
  309.4 94.8 reduce-scatter.10
  407.7 95.1 reduce-scatter.8
  505.4 46.9 all-reduce.12
